TPU v7x, 512 devices: a whole 4x4x16 slice. The times are simulated.
512 devices in a mesh: ctx: 16 (over y, x_hi, core), fsdp: 32 (over z, x_lo).
Axes of the slice: x: 4 (x_hi: 2, x_lo: 2; x = x_hi * 2 + x_lo), y: 4, z: 16, core: 2. Of those that a mesh axis runs over, the one named last changes fastest.
Arguments:
- query_states: bfloat16 [32, 2048, 2048], P('fsdp', 'ctx'), may hold values from -12 to 12
- key_states: bfloat16 [32, 2048, 512], P('fsdp', 'ctx'), may hold values from -24 to 24
- value_states: bfloat16 [32, 2048, 512], P('fsdp', 'ctx'), may hold values from -170 to 170
- doc_ids: int32 [32, 2048], P('fsdp', 'ctx'), may hold values from 0 to 7, never falling along the last dimension, each value on 1 to 1536 neighbouring positions
- routes: int32 [32, 2048, 2], P('fsdp', 'ctx'), may hold values from 0 to 7, as said below
- route_weight: bfloat16 [32, 2048, 2], P('fsdp', 'ctx'), may hold values from 0.19921875 to 1
- cotangent: bfloat16 [32, 2048, 2048], P('fsdp', 'ctx'), may hold values from -6 to 6
- gate_weight: bfloat16 [2048, 7168], P('fsdp', 'ctx'), may hold values from -0.125 to 0.125
- up_weight: bfloat16 [2048, 7168], P('fsdp', 'ctx'), may hold values from -0.125 to 0.125
- down_weight: bfloat16 [7168, 2048], P('ctx', 'fsdp'), may hold values from -0.0625 to 0.0625
Outputs:
- attn_out: bfloat16 [32, 2048, 2048], P('fsdp', 'ctx')
- d_input: bfloat16 [32, 2048, 2048], P('fsdp', 'ctx')
Inputs may be any that keep to these rules, and one draw needn't show every extreme that they name: `routes`: each token names 2 different experts. Of the 128 tokens of one block of a sequence, at most 8 name expert 0; in some sequence every block has exactly 8 such tokens.
All inputs are finite; a program needn't handle non-finite values.
Results may differ from a plain program's by a relative error of at most 0.02.
Values may be sent and summed in bfloat16 or wider, within the bound.
No kernel may reach another device: no remote copies, remote signals or barrier semaphores. Data moves between devices by JAX's collectives and lax.ppermute only.
A program may use at most 64 MiB of HBM per device.

v0:
```python
import jax
import jax.numpy as jnp
from jax import lax
from jax.sharding import PartitionSpec as P

HEADS = 16
KV_HEADS = 4
HEAD_DIM = 128
CAP = 8


epsilon = 1e-05
far_below = -1e30


def from_behind(shard, axis, by):
    length = lax.axis_size(axis)
    return lax.ppermute(shard, axis, [(i, (i + by) % length) for i in range(length)])


def on_device(
    query_states,
    key_states,
    value_states,
    doc_ids,
    routes,
    route_weight,
    cotangent,
    gate_weight,
    up_weight,
    down_weight,
):
    gate_panel, up_panel, down_panel = (
        lax.all_gather(gate_weight, "fsdp", axis=0, tiled=True),
        lax.all_gather(up_weight, "fsdp", axis=0, tiled=True),
        lax.all_gather(down_weight, "fsdp", axis=1, tiled=True),
    )
    every_doc = lax.all_gather(doc_ids, "ctx", axis=1, tiled=True)[0]
    cycle_size = lax.axis_size("ctx")
    position = lax.axis_index("ctx")
    tok_count = query_states.shape[1]
    model_width = query_states.shape[2]
    group_size = HEADS // KV_HEADS
    scaling = HEAD_DIM ** (-0.5)
    query_heads = query_states[0].reshape(tok_count, KV_HEADS, group_size, HEAD_DIM)
    query_docs = lax.dynamic_slice_in_dim(every_doc, position * tok_count, tok_count)

    def attend_block(running, key_block, source):
        key_heads = key_block[0].reshape(tok_count, KV_HEADS, HEAD_DIM)
        value_heads = key_block[1].reshape(tok_count, KV_HEADS, HEAD_DIM)
        key_docs = lax.dynamic_slice_in_dim(every_doc, source * tok_count, tok_count)
        allowed = key_docs[None, :] == query_docs[:, None]
        row_max, row_total, weighted = running
        scores = (
            jnp.einsum("igrd,jgd->grij", query_heads, key_heads, preferred_element_type=jnp.float32)
            * scaling
        )
        masked = jnp.where(allowed, scores, far_below)
        new_max = jnp.maximum(row_max, jnp.max(masked, axis=-1))
        unscaled = jnp.where(allowed, jnp.exp(masked - new_max[..., None]), 0.0)
        factor = jnp.exp(row_max - new_max)
        probabilities = unscaled.astype(jnp.bfloat16)
        weighted = weighted * factor[..., None] + jnp.einsum(
            "grij,jgd->grid", probabilities, value_heads, preferred_element_type=jnp.float32
        )
        return (new_max, row_total * factor + jnp.sum(unscaled, axis=-1), weighted)

    own_block = (key_states[0], value_states[0])
    start_state = (
        jnp.full((KV_HEADS, group_size, tok_count), far_below, jnp.float32),
        jnp.zeros((KV_HEADS, group_size, tok_count), jnp.float32),
        jnp.zeros((KV_HEADS, group_size, tok_count, HEAD_DIM), jnp.float32),
    )
    running = attend_block(start_state, own_block, position)

    def cycle_step(step_index, loop_state):
        running_now, key_block = loop_state
        key_block = from_behind((key_block[0], key_block[1]), "ctx", 1)
        return (
            attend_block(running_now, key_block, (position - step_index) % cycle_size),
            key_block,
        )

    running, last_block = lax.fori_loop(1, cycle_size, cycle_step, (running, own_block))
    row_max, row_total, weighted = running
    mixed = weighted / row_total[..., None]
    attn_out = (
        jnp.transpose(mixed, (2, 0, 1, 3)).reshape(tok_count, model_width).astype(jnp.bfloat16)
    )
    as_float = attn_out.astype(jnp.float32)
    inverse = lax.rsqrt(jnp.mean(as_float * as_float, axis=-1, keepdims=True) + epsilon)
    scaled = as_float * inverse
    normed = scaled.astype(jnp.bfloat16)
    chosen = routes[0] == 0
    routed = jnp.any(chosen, axis=-1)
    weight = jnp.sum(jnp.where(chosen, route_weight[0].astype(jnp.float32), 0.0), axis=-1)
    slot_index = jnp.cumsum(routed.astype(jnp.int32)) - 1
    selector = (slot_index[None, :] == jnp.arange(CAP, dtype=jnp.int32)[:, None]) & routed[None, :]
    selector_half = selector.astype(jnp.bfloat16)
    selector_float = selector.astype(jnp.float32)
    slot_x = jnp.dot(selector_half, normed, preferred_element_type=jnp.float32).astype(jnp.bfloat16)
    slot_dy = jnp.dot(selector_half, cotangent[0], preferred_element_type=jnp.float32).astype(
        jnp.bfloat16
    )
    slot_w = jnp.dot(selector_float, weight, precision=lax.Precision.HIGHEST).astype(jnp.bfloat16)
    rows_x, rows_dy, rows_w = (
        lax.all_gather(slot_x, "ctx", axis=0, tiled=True),
        lax.all_gather(slot_dy, "ctx", axis=0, tiled=True),
        lax.all_gather(slot_w, "ctx", axis=0, tiled=True),
    )
    contract_last = (((1,), (1,)), ((), ()))
    gate_proj = jnp.dot(rows_x, gate_panel, preferred_element_type=jnp.float32)
    up_proj = jnp.dot(rows_x, up_panel, preferred_element_type=jnp.float32)
    back_grad = lax.dot_general(
        rows_dy, down_panel, contract_last, preferred_element_type=jnp.float32
    )
    back_grad = back_grad * rows_w.astype(jnp.float32)[:, None]
    sigmoid_gate = jax.nn.sigmoid(gate_proj)
    grad_gate = (
        back_grad * up_proj * sigmoid_gate * (1.0 + gate_proj * (1.0 - sigmoid_gate))
    ).astype(jnp.bfloat16)
    grad_up = (back_grad * gate_proj * sigmoid_gate).astype(jnp.bfloat16)
    result = lax.dot_general(
        grad_gate, gate_panel, contract_last, preferred_element_type=jnp.float32
    )
    d_slots = lax.psum_scatter(
        (
            result
            + lax.dot_general(grad_up, up_panel, contract_last, preferred_element_type=jnp.float32)
        ).astype(jnp.bfloat16),
        "ctx",
        scatter_dimension=0,
        tiled=True,
    ).astype(jnp.float32)
    d_norm = jnp.dot(selector_float.T, d_slots, precision=lax.Precision.HIGHEST)
    d_input = inverse * (d_norm - scaled * jnp.mean(d_norm * scaled, axis=-1, keepdims=True))
    return (attn_out[None], d_input.astype(jnp.bfloat16)[None])


def solution(mesh):
    return jax.shard_map(
        on_device,
        mesh=mesh,
        in_specs=(
            P("fsdp", "ctx", None),
            P("fsdp", "ctx", None),
            P("fsdp", "ctx", None),
            P("fsdp", "ctx"),
            P("fsdp", "ctx", None),
            P("fsdp", "ctx", None),
            P("fsdp", "ctx", None),
            P("fsdp", "ctx"),
            P("fsdp", "ctx"),
            P("ctx", "fsdp"),
        ),
        out_specs=(P("fsdp", "ctx", None), P("fsdp", "ctx", None)),
        check_vma=False,
    )
```

profile of v0, /device:TPU:1, one launch (start us, length us, event | category | flops | bytes accessed | tf_op | source)
XLA Modules:
  0.0 520.1 jit_solution(569136732008379769)
XLA Ops:
  13.4 25.9 %all_gather.21 = s32[1,2048]{1,0:T(1,128)S(1)} all-gather(s32[1,128]{1,0:T(1,128)} %param.15), channel_id=1, replica_groups=mesh['ctx'=16,'fsdp'=32] {'ctx'}, dimensions={1}, use_global_device_ids=true | all-gather | bytes 8704 | tf_op jit(solution)/shard_map/all_gather | solution.py:38
  39.4 1.3 copy.22
  42.1 198.4 %while.23 = (s32[]{:T(128)}, f32[4,4,128]{2,1,0:T(4,128)S(1)}, f32[4,4,128]{2,1,0:T(4,128)S(1)}, f32[4,4,128,128]{3,2,1,0:T(8,128)S(1)}, bf16[128,512]{0,1:T(8,1...) while((s32[]{:T(128)}, f32[4,4,128]{2,1,0:T(4,128)S(1)}, ...), condition=%wide.region_5.6_spmd, body=%wide.region_2.5_spmd.sunk | while | flops 137121808 | bytes 7801232 | solution.py:84
  42.1 5.1 collective-permute-start
  47.2 2.3 collective-permute-start.1
  50.3 1.7 collective-permute-done.1
  52.8 5.9 %collective-permute-start = (bf16[128,512]{0,1:T(8,128)(2,1)S(1)}, bf16[128,512]{0,1:T(8,128)(2,1)S(1)}, u32[]{:S(2)}, u32[]{:S(2)}) collective-permute-start(bf16[128,512]{0,1:T(8,128)(2,1)S(1)} %get-tuple-element.383), channel_id=1, source_target_pairs={{0,32},{32,64},{64,96},{96,128},{128,160},{160,192},{192,224},{224... | collective-permute-start | bytes 393224 | tf_op jit(solution)/shard_map/while/body/eval_jaxpr/ppermute | solution.py:18
  58.7 1.9 collective-permute-start.1
  62.0 1.7 collective-permute-done.1
  64.5 6.2 %collective-permute-start = (bf16[128,512]{0,1:T(8,128)(2,1)S(1)}, bf16[128,512]{0,1:T(8,128)(2,1)S(1)}, u32[]{:S(2)}, u32[]{:S(2)}) collective-permute-start(bf16[128,512]{0,1:T(8,128)(2,1)S(1)} %get-tuple-element.383), channel_id=1, source_target_pairs={{0,32},{32,64},{64,96},{96,128},{128,160},{160,192},{192,224},{224... | collective-permute-start | bytes 393224 | tf_op jit(solution)/shard_map/while/body/eval_jaxpr/ppermute | solution.py:18
  70.7 1.9 collective-permute-start.1
  74.2 1.5 collective-permute-done.1
  76.5 5.9 %collective-permute-start = (bf16[128,512]{0,1:T(8,128)(2,1)S(1)}, bf16[128,512]{0,1:T(8,128)(2,1)S(1)}, u32[]{:S(2)}, u32[]{:S(2)}) collective-permute-start(bf16[128,512]{0,1:T(8,128)(2,1)S(1)} %get-tuple-element.383), channel_id=1, source_target_pairs={{0,32},{32,64},{64,96},{96,128},{128,160},{160,192},{192,224},{224... | collective-permute-start | bytes 393224 | tf_op jit(solution)/shard_map/while/body/eval_jaxpr/ppermute | solution.py:18
  82.4 1.9 collective-permute-start.1
  84.5 2.9 collective-permute-done
  90.1 4.3 collective-permute-start
  94.4 1.9 collective-permute-start.1
  96.5 5.3 %collective-permute-done = bf16[128,512]{0,1:T(8,128)(2,1)S(1)} collective-permute-done((bf16[128,512]{0,1:T(8,128)(2,1)S(1)}, bf16[128,512]{0,1:T(8,128)(2,1)S(1)}, u32[]{:S(2)}, u32[]{:S(2)}) %collective-permute-start) | collective-permute-done | bytes 131104 | tf_op jit(solution)/shard_map/while/body/eval_jaxpr/ppermute | solution.py:18
  104.5 1.9 collective-permute-start
  106.5 1.9 collective-permute-start.1
  108.6 7.3 %collective-permute-done = bf16[128,512]{0,1:T(8,128)(2,1)S(1)} collective-permute-done((bf16[128,512]{0,1:T(8,128)(2,1)S(1)}, bf16[128,512]{0,1:T(8,128)(2,1)S(1)}, u32[]{:S(2)}, u32[]{:S(2)}) %collective-permute-start) | collective-permute-done | bytes 131104 | tf_op jit(solution)/shard_map/while/body/eval_jaxpr/ppermute | solution.py:18
  116.5 1.3 collective-permute-done.1
  118.5 1.9 collective-permute-start
  120.4 1.9 collective-permute-start.1
  122.5 7.3 %collective-permute-done = bf16[128,512]{0,1:T(8,128)(2,1)S(1)} collective-permute-done((bf16[128,512]{0,1:T(8,128)(2,1)S(1)}, bf16[128,512]{0,1:T(8,128)(2,1)S(1)}, u32[]{:S(2)}, u32[]{:S(2)}) %collective-permute-start) | collective-permute-done | bytes 131104 | tf_op jit(solution)/shard_map/while/body/eval_jaxpr/ppermute | solution.py:18
  132.5 1.9 collective-permute-start
  134.5 1.9 collective-permute-start.1
  136.6 6.3 %collective-permute-done = bf16[128,512]{0,1:T(8,128)(2,1)S(1)} collective-permute-done((bf16[128,512]{0,1:T(8,128)(2,1)S(1)}, bf16[128,512]{0,1:T(8,128)(2,1)S(1)}, u32[]{:S(2)}, u32[]{:S(2)}) %collective-permute-start) | collective-permute-done | bytes 131104 | tf_op jit(solution)/shard_map/while/body/eval_jaxpr/ppermute | solution.py:18
  143.5 1.3 collective-permute-done.1
  145.5 1.9 collective-permute-start
  147.5 1.9 collective-permute-start.1
  149.6 6.1 %collective-permute-done = bf16[128,512]{0,1:T(8,128)(2,1)S(1)} collective-permute-done((bf16[128,512]{0,1:T(8,128)(2,1)S(1)}, bf16[128,512]{0,1:T(8,128)(2,1)S(1)}, u32[]{:S(2)}, u32[]{:S(2)}) %collective-permute-start) | collective-permute-done | bytes 131104 | tf_op jit(solution)/shard_map/while/body/eval_jaxpr/ppermute | solution.py:18
  156.3 1.3 collective-permute-done.1
  158.4 1.9 collective-permute-start
  160.3 1.9 collective-permute-start.1
  162.4 5.8 %collective-permute-done = bf16[128,512]{0,1:T(8,128)(2,1)S(1)} collective-permute-done((bf16[128,512]{0,1:T(8,128)(2,1)S(1)}, bf16[128,512]{0,1:T(8,128)(2,1)S(1)}, u32[]{:S(2)}, u32[]{:S(2)}) %collective-permute-start) | collective-permute-done | bytes 131104 | tf_op jit(solution)/shard_map/while/body/eval_jaxpr/ppermute | solution.py:18
  170.9 1.9 collective-permute-start
  172.8 1.9 collective-permute-start.1
  175.0 6.8 %collective-permute-done = bf16[128,512]{0,1:T(8,128)(2,1)S(1)} collective-permute-done((bf16[128,512]{0,1:T(8,128)(2,1)S(1)}, bf16[128,512]{0,1:T(8,128)(2,1)S(1)}, u32[]{:S(2)}, u32[]{:S(2)}) %collective-permute-start) | collective-permute-done | bytes 131104 | tf_op jit(solution)/shard_map/while/body/eval_jaxpr/ppermute | solution.py:18
  184.4 1.9 collective-permute-start
  186.3 1.9 collective-permute-start.1
  188.4 7.1 %collective-permute-done = bf16[128,512]{0,1:T(8,128)(2,1)S(1)} collective-permute-done((bf16[128,512]{0,1:T(8,128)(2,1)S(1)}, bf16[128,512]{0,1:T(8,128)(2,1)S(1)}, u32[]{:S(2)}, u32[]{:S(2)}) %collective-permute-start) | collective-permute-done | bytes 131104 | tf_op jit(solution)/shard_map/while/body/eval_jaxpr/ppermute | solution.py:18
  198.2 1.9 collective-permute-start
  200.1 1.9 collective-permute-start.1
  202.2 7.9 %collective-permute-done = bf16[128,512]{0,1:T(8,128)(2,1)S(1)} collective-permute-done((bf16[128,512]{0,1:T(8,128)(2,1)S(1)}, bf16[128,512]{0,1:T(8,128)(2,1)S(1)}, u32[]{:S(2)}, u32[]{:S(2)}) %collective-permute-start) | collective-permute-done | bytes 131104 | tf_op jit(solution)/shard_map/while/body/eval_jaxpr/ppermute | solution.py:18
  210.7 1.3 collective-permute-done.1
  212.8 1.9 collective-permute-start
  214.7 1.9 collective-permute-start.1
  216.8 7.4 %collective-permute-done = bf16[128,512]{0,1:T(8,128)(2,1)S(1)} collective-permute-done((bf16[128,512]{0,1:T(8,128)(2,1)S(1)}, bf16[128,512]{0,1:T(8,128)(2,1)S(1)}, u32[]{:S(2)}, u32[]{:S(2)}) %collective-permute-start) | collective-permute-done | bytes 131104 | tf_op jit(solution)/shard_map/while/body/eval_jaxpr/ppermute | solution.py:18
  224.8 1.3 collective-permute-done.1
  226.8 1.9 collective-permute-start
  228.7 1.9 collective-permute-start.1
  230.9 7.0 %collective-permute-done = bf16[128,512]{0,1:T(8,128)(2,1)S(1)} collective-permute-done((bf16[128,512]{0,1:T(8,128)(2,1)S(1)}, bf16[128,512]{0,1:T(8,128)(2,1)S(1)}, u32[]{:S(2)}, u32[]{:S(2)}) %collective-permute-start) | collective-permute-done | bytes 131104 | tf_op jit(solution)/shard_map/while/body/eval_jaxpr/ppermute | solution.py:18
  241.1 1.7 copy.32
  242.8 1.6 reshape.107
  247.2 41.1 %all-reduce = bf16[128]{0:T(256)(128)(2,1)S(1)} all-reduce(bf16[128]{0:T(256)(128)(2,1)S(1)} %dynamic-update-slice), channel_id=1, replica_groups=mesh['ctx'=16,'fsdp'=32] {'ctx'}, use_global_device_ids=true, to_apply=%add | all-reduce | flops 128 | bytes 512
  288.7 23.5 %all_gather.25 = bf16[128,2048]{1,0:T(8,128)(2,1)S(1)} all-gather(bf16[8,2048]{1,0:T(8,128)(2,1)S(1)} %convolution_convert_fusion), channel_id=1, replica_groups=mesh['ctx'=16,'fsdp'=32] {'ctx'}, dimensions={0}, use_global_device_ids=true | all-gather | bytes 557056 | tf_op jit(solution)/shard_map/all_gather | solution.py:107
  312.2 26.3 %all_gather.22 = bf16[128,2048]{1,0:T(8,128)(2,1)S(1)} all-gather(bf16[8,2048]{1,0:T(8,128)(2,1)S(1)} %convolution_convert_fusion.1), channel_id=1, replica_groups=mesh['ctx'=16,'fsdp'=32] {'ctx'}, dimensions={0}, use_global_device_ids=true | all-gather | bytes 557056 | tf_op jit(solution)/shard_map/all_gather | solution.py:108
  338.5 3.2 fusion.55
  341.7 2.5 convolution_multiply_fusion.3
  344.2 52.3 %all-gather.6.cloned.1.call-done = bf16[2048,448]{1,0:T(8,128)(2,1)} async-done(((bf16[64,448]{1,0:T(8,128)(2,1)}), bf16[2048,448]{1,0:T(8,128)(2,1)}) %all-gather.6.cloned.1.call-update) | async-done | bytes 1835024 | tf_op jit(solution)/shard_map/all_gather | solution.py:35
  396.5 5.5 %fusion.15 = f32[128,2048]{1,0:T(8,128)} fusion(bf16[2048,448]{1,0:T(8,128)(2,1)} %all-gather.8.cloned.1.call-done, f32[128,448]{0,1:T(8,128)S(1)} %convolution_multiply_fusion.3, bf16[128,2048]{1,0:T(8,128)(2,1)S(1)} %all_gather.25, bf16[2048,448]{1,0:T(8,128)(2,1)} %all-gather.6.cloned.1.call-done, f32[128,448]{0,1:T(8,128)} %fusion.55), kind=kOutput, calls=%fused_computation.27 | convolution fusion | flops 470335488 | bytes 5701632 | tf_op jit(solution)/shard_map/dot_general | solution.py:123
  402.0 3.5 fusion.9
  407.1 104.2 %reduce-scatter.2.cloned.1.call-done = bf16[8,2048]{1,0:T(8,128)(2,1)} async-done(((bf16[128,2048]{1,0:T(8,128)(2,1)}), bf16[8,2048]{1,0:T(8,128)(2,1)}) %reduce-scatter.2.cloned.1.call-update) | async-done | bytes 32784 | tf_op jit(solution)/shard_map/reduce_scatter | solution.py:126
  (211 shorter events, 46.8 us)
Async XLA Ops:
  7.2 281.1 %copy-start = (bf16[1,128,2048]{2,1,0:T(8,128)(2,1)S(1)}, bf16[1,128,2048]{2,1,0:T(8,128)(2,1)}, u32[]{:S(2)}) copy-start(bf16[1,128,2048]{2,1,0:T(8,128)(2,1)} %param.18) | copy-start | bytes 1572868
  7.2 331.3 %all-gather.8.cloned.1.call-start = ((), (), s32[]{:S(2)}) async-start(), calls=%async_computation.3 | async-start | bytes 2162688 | tf_op jit(solution)/shard_map/all_gather | solution.py:34
  7.9 333.8 %all-gather.4.cloned.1.call-start = ((), (), s32[]{:S(2)}) async-start(), calls=%async_computation.1 | async-start | bytes 2162688 | tf_op jit(solution)/shard_map/all_gather | solution.py:36
  8.7 387.8 %all-gather.6.cloned.1.call-start = ((), (), s32[]{:S(2)}) async-start(), calls=%async_computation.2 | async-start | bytes 2162688 | tf_op jit(solution)/shard_map/all_gather | solution.py:35
  9.4 501.9 %reduce-scatter.2.cloned.1.call-start = ((), (), s32[]{:S(2)}) async-start(), calls=%async_computation.4 | async-start | bytes 557056 | tf_op jit(solution)/shard_map/reduce_scatter | solution.py:126
  42.1 7.6 %collective-permute-start = (bf16[128,512]{0,1:T(8,128)(2,1)S(1)}, bf16[128,512]{0,1:T(8,128)(2,1)S(1)}, u32[]{:S(2)}, u32[]{:S(2)}) collective-permute-start(bf16[128,512]{0,1:T(8,128)(2,1)S(1)} %get-tuple-element.383), channel_id=1, source_target_pairs={{0,32},{32,64},{64,96},{96,128},{128,160},{160,192},{192,224},{224... | collective-permute-start | bytes 393224 | tf_op jit(solution)/shard_map/while/body/eval_jaxpr/ppermute | solution.py:18
  47.2 4.9 collective-permute-start.1
  52.8 8.6 %collective-permute-start = (bf16[128,512]{0,1:T(8,128)(2,1)S(1)}, bf16[128,512]{0,1:T(8,128)(2,1)S(1)}, u32[]{:S(2)}, u32[]{:S(2)}) collective-permute-start(bf16[128,512]{0,1:T(8,128)(2,1)S(1)} %get-tuple-element.383), channel_id=1, source_target_pairs={{0,32},{32,64},{64,96},{96,128},{128,160},{160,192},{192,224},{224... | collective-permute-start | bytes 393224 | tf_op jit(solution)/shard_map/while/body/eval_jaxpr/ppermute | solution.py:18
  58.7 5.0 collective-permute-start.1
  64.5 9.1 %collective-permute-start = (bf16[128,512]{0,1:T(8,128)(2,1)S(1)}, bf16[128,512]{0,1:T(8,128)(2,1)S(1)}, u32[]{:S(2)}, u32[]{:S(2)}) collective-permute-start(bf16[128,512]{0,1:T(8,128)(2,1)S(1)} %get-tuple-element.383), channel_id=1, source_target_pairs={{0,32},{32,64},{64,96},{96,128},{128,160},{160,192},{192,224},{224... | collective-permute-start | bytes 393224 | tf_op jit(solution)/shard_map/while/body/eval_jaxpr/ppermute | solution.py:18
  70.7 5.1 collective-permute-start.1
  76.5 11.0 %collective-permute-start = (bf16[128,512]{0,1:T(8,128)(2,1)S(1)}, bf16[128,512]{0,1:T(8,128)(2,1)S(1)}, u32[]{:S(2)}, u32[]{:S(2)}) collective-permute-start(bf16[128,512]{0,1:T(8,128)(2,1)S(1)} %get-tuple-element.383), channel_id=1, source_target_pairs={{0,32},{32,64},{64,96},{96,128},{128,160},{160,192},{192,224},{224... | collective-permute-start | bytes 393224 | tf_op jit(solution)/shard_map/while/body/eval_jaxpr/ppermute | solution.py:18
  82.4 7.0 %collective-permute-start.1 = (bf16[128,512]{0,1:T(8,128)(2,1)S(1)}, bf16[128,512]{0,1:T(8,128)(2,1)S(1)}, u32[]{:S(2)}, u32[]{:S(2)}) collective-permute-start(bf16[128,512]{0,1:T(8,128)(2,1)S(1)} %get-tuple-element.384), channel_id=1, source_target_pairs={{0,32},{32,64},{64,96},{96,128},{128,160},{160,192},{192,224},{224... | collective-permute-start | bytes 393224 | tf_op jit(solution)/shard_map/while/body/eval_jaxpr/ppermute | solution.py:18
  90.1 11.8 %collective-permute-start = (bf16[128,512]{0,1:T(8,128)(2,1)S(1)}, bf16[128,512]{0,1:T(8,128)(2,1)S(1)}, u32[]{:S(2)}, u32[]{:S(2)}) collective-permute-start(bf16[128,512]{0,1:T(8,128)(2,1)S(1)} %get-tuple-element.383), channel_id=1, source_target_pairs={{0,32},{32,64},{64,96},{96,128},{128,160},{160,192},{192,224},{224... | collective-permute-start | bytes 393224 | tf_op jit(solution)/shard_map/while/body/eval_jaxpr/ppermute | solution.py:18
  94.4 9.4 %collective-permute-start.1 = (bf16[128,512]{0,1:T(8,128)(2,1)S(1)}, bf16[128,512]{0,1:T(8,128)(2,1)S(1)}, u32[]{:S(2)}, u32[]{:S(2)}) collective-permute-start(bf16[128,512]{0,1:T(8,128)(2,1)S(1)} %get-tuple-element.384), channel_id=1, source_target_pairs={{0,32},{32,64},{64,96},{96,128},{128,160},{160,192},{192,224},{224... | collective-permute-start | bytes 393224 | tf_op jit(solution)/shard_map/while/body/eval_jaxpr/ppermute | solution.py:18
  104.5 11.3 %collective-permute-start = (bf16[128,512]{0,1:T(8,128)(2,1)S(1)}, bf16[128,512]{0,1:T(8,128)(2,1)S(1)}, u32[]{:S(2)}, u32[]{:S(2)}) collective-permute-start(bf16[128,512]{0,1:T(8,128)(2,1)S(1)} %get-tuple-element.383), channel_id=1, source_target_pairs={{0,32},{32,64},{64,96},{96,128},{128,160},{160,192},{192,224},{224... | collective-permute-start | bytes 393224 | tf_op jit(solution)/shard_map/while/body/eval_jaxpr/ppermute | solution.py:18
  106.5 11.3 %collective-permute-start.1 = (bf16[128,512]{0,1:T(8,128)(2,1)S(1)}, bf16[128,512]{0,1:T(8,128)(2,1)S(1)}, u32[]{:S(2)}, u32[]{:S(2)}) collective-permute-start(bf16[128,512]{0,1:T(8,128)(2,1)S(1)} %get-tuple-element.384), channel_id=1, source_target_pairs={{0,32},{32,64},{64,96},{96,128},{128,160},{160,192},{192,224},{224... | collective-permute-start | bytes 393224 | tf_op jit(solution)/shard_map/while/body/eval_jaxpr/ppermute | solution.py:18
  118.5 11.4 %collective-permute-start = (bf16[128,512]{0,1:T(8,128)(2,1)S(1)}, bf16[128,512]{0,1:T(8,128)(2,1)S(1)}, u32[]{:S(2)}, u32[]{:S(2)}) collective-permute-start(bf16[128,512]{0,1:T(8,128)(2,1)S(1)} %get-tuple-element.383), channel_id=1, source_target_pairs={{0,32},{32,64},{64,96},{96,128},{128,160},{160,192},{192,224},{224... | collective-permute-start | bytes 393224 | tf_op jit(solution)/shard_map/while/body/eval_jaxpr/ppermute | solution.py:18
  120.4 11.4 %collective-permute-start.1 = (bf16[128,512]{0,1:T(8,128)(2,1)S(1)}, bf16[128,512]{0,1:T(8,128)(2,1)S(1)}, u32[]{:S(2)}, u32[]{:S(2)}) collective-permute-start(bf16[128,512]{0,1:T(8,128)(2,1)S(1)} %get-tuple-element.384), channel_id=1, source_target_pairs={{0,32},{32,64},{64,96},{96,128},{128,160},{160,192},{192,224},{224... | collective-permute-start | bytes 393224 | tf_op jit(solution)/shard_map/while/body/eval_jaxpr/ppermute | solution.py:18
  132.5 10.3 %collective-permute-start = (bf16[128,512]{0,1:T(8,128)(2,1)S(1)}, bf16[128,512]{0,1:T(8,128)(2,1)S(1)}, u32[]{:S(2)}, u32[]{:S(2)}) collective-permute-start(bf16[128,512]{0,1:T(8,128)(2,1)S(1)} %get-tuple-element.383), channel_id=1, source_target_pairs={{0,32},{32,64},{64,96},{96,128},{128,160},{160,192},{192,224},{224... | collective-permute-start | bytes 393224 | tf_op jit(solution)/shard_map/while/body/eval_jaxpr/ppermute | solution.py:18
  134.5 10.3 %collective-permute-start.1 = (bf16[128,512]{0,1:T(8,128)(2,1)S(1)}, bf16[128,512]{0,1:T(8,128)(2,1)S(1)}, u32[]{:S(2)}, u32[]{:S(2)}) collective-permute-start(bf16[128,512]{0,1:T(8,128)(2,1)S(1)} %get-tuple-element.384), channel_id=1, source_target_pairs={{0,32},{32,64},{64,96},{96,128},{128,160},{160,192},{192,224},{224... | collective-permute-start | bytes 393224 | tf_op jit(solution)/shard_map/while/body/eval_jaxpr/ppermute | solution.py:18
  145.5 10.2 %collective-permute-start = (bf16[128,512]{0,1:T(8,128)(2,1)S(1)}, bf16[128,512]{0,1:T(8,128)(2,1)S(1)}, u32[]{:S(2)}, u32[]{:S(2)}) collective-permute-start(bf16[128,512]{0,1:T(8,128)(2,1)S(1)} %get-tuple-element.383), channel_id=1, source_target_pairs={{0,32},{32,64},{64,96},{96,128},{128,160},{160,192},{192,224},{224... | collective-permute-start | bytes 393224 | tf_op jit(solution)/shard_map/while/body/eval_jaxpr/ppermute | solution.py:18
  147.5 10.2 %collective-permute-start.1 = (bf16[128,512]{0,1:T(8,128)(2,1)S(1)}, bf16[128,512]{0,1:T(8,128)(2,1)S(1)}, u32[]{:S(2)}, u32[]{:S(2)}) collective-permute-start(bf16[128,512]{0,1:T(8,128)(2,1)S(1)} %get-tuple-element.384), channel_id=1, source_target_pairs={{0,32},{32,64},{64,96},{96,128},{128,160},{160,192},{192,224},{224... | collective-permute-start | bytes 393224 | tf_op jit(solution)/shard_map/while/body/eval_jaxpr/ppermute | solution.py:18
  158.4 9.9 %collective-permute-start = (bf16[128,512]{0,1:T(8,128)(2,1)S(1)}, bf16[128,512]{0,1:T(8,128)(2,1)S(1)}, u32[]{:S(2)}, u32[]{:S(2)}) collective-permute-start(bf16[128,512]{0,1:T(8,128)(2,1)S(1)} %get-tuple-element.383), channel_id=1, source_target_pairs={{0,32},{32,64},{64,96},{96,128},{128,160},{160,192},{192,224},{224... | collective-permute-start | bytes 393224 | tf_op jit(solution)/shard_map/while/body/eval_jaxpr/ppermute | solution.py:18
  160.3 9.9 %collective-permute-start.1 = (bf16[128,512]{0,1:T(8,128)(2,1)S(1)}, bf16[128,512]{0,1:T(8,128)(2,1)S(1)}, u32[]{:S(2)}, u32[]{:S(2)}) collective-permute-start(bf16[128,512]{0,1:T(8,128)(2,1)S(1)} %get-tuple-element.384), channel_id=1, source_target_pairs={{0,32},{32,64},{64,96},{96,128},{128,160},{160,192},{192,224},{224... | collective-permute-start | bytes 393224 | tf_op jit(solution)/shard_map/while/body/eval_jaxpr/ppermute | solution.py:18
  170.9 10.8 %collective-permute-start = (bf16[128,512]{0,1:T(8,128)(2,1)S(1)}, bf16[128,512]{0,1:T(8,128)(2,1)S(1)}, u32[]{:S(2)}, u32[]{:S(2)}) collective-permute-start(bf16[128,512]{0,1:T(8,128)(2,1)S(1)} %get-tuple-element.383), channel_id=1, source_target_pairs={{0,32},{32,64},{64,96},{96,128},{128,160},{160,192},{192,224},{224... | collective-permute-start | bytes 393224 | tf_op jit(solution)/shard_map/while/body/eval_jaxpr/ppermute | solution.py:18
  172.8 10.8 %collective-permute-start.1 = (bf16[128,512]{0,1:T(8,128)(2,1)S(1)}, bf16[128,512]{0,1:T(8,128)(2,1)S(1)}, u32[]{:S(2)}, u32[]{:S(2)}) collective-permute-start(bf16[128,512]{0,1:T(8,128)(2,1)S(1)} %get-tuple-element.384), channel_id=1, source_target_pairs={{0,32},{32,64},{64,96},{96,128},{128,160},{160,192},{192,224},{224... | collective-permute-start | bytes 393224 | tf_op jit(solution)/shard_map/while/body/eval_jaxpr/ppermute | solution.py:18
  184.4 11.1 %collective-permute-start = (bf16[128,512]{0,1:T(8,128)(2,1)S(1)}, bf16[128,512]{0,1:T(8,128)(2,1)S(1)}, u32[]{:S(2)}, u32[]{:S(2)}) collective-permute-start(bf16[128,512]{0,1:T(8,128)(2,1)S(1)} %get-tuple-element.383), channel_id=1, source_target_pairs={{0,32},{32,64},{64,96},{96,128},{128,160},{160,192},{192,224},{224... | collective-permute-start | bytes 393224 | tf_op jit(solution)/shard_map/while/body/eval_jaxpr/ppermute | solution.py:18
  186.3 11.1 %collective-permute-start.1 = (bf16[128,512]{0,1:T(8,128)(2,1)S(1)}, bf16[128,512]{0,1:T(8,128)(2,1)S(1)}, u32[]{:S(2)}, u32[]{:S(2)}) collective-permute-start(bf16[128,512]{0,1:T(8,128)(2,1)S(1)} %get-tuple-element.384), channel_id=1, source_target_pairs={{0,32},{32,64},{64,96},{96,128},{128,160},{160,192},{192,224},{224... | collective-permute-start | bytes 393224 | tf_op jit(solution)/shard_map/while/body/eval_jaxpr/ppermute | solution.py:18
  198.2 11.9 %collective-permute-start = (bf16[128,512]{0,1:T(8,128)(2,1)S(1)}, bf16[128,512]{0,1:T(8,128)(2,1)S(1)}, u32[]{:S(2)}, u32[]{:S(2)}) collective-permute-start(bf16[128,512]{0,1:T(8,128)(2,1)S(1)} %get-tuple-element.383), channel_id=1, source_target_pairs={{0,32},{32,64},{64,96},{96,128},{128,160},{160,192},{192,224},{224... | collective-permute-start | bytes 393224 | tf_op jit(solution)/shard_map/while/body/eval_jaxpr/ppermute | solution.py:18
  200.1 11.9 %collective-permute-start.1 = (bf16[128,512]{0,1:T(8,128)(2,1)S(1)}, bf16[128,512]{0,1:T(8,128)(2,1)S(1)}, u32[]{:S(2)}, u32[]{:S(2)}) collective-permute-start(bf16[128,512]{0,1:T(8,128)(2,1)S(1)} %get-tuple-element.384), channel_id=1, source_target_pairs={{0,32},{32,64},{64,96},{96,128},{128,160},{160,192},{192,224},{224... | collective-permute-start | bytes 393224 | tf_op jit(solution)/shard_map/while/body/eval_jaxpr/ppermute | solution.py:18
  212.8 11.4 %collective-permute-start = (bf16[128,512]{0,1:T(8,128)(2,1)S(1)}, bf16[128,512]{0,1:T(8,128)(2,1)S(1)}, u32[]{:S(2)}, u32[]{:S(2)}) collective-permute-start(bf16[128,512]{0,1:T(8,128)(2,1)S(1)} %get-tuple-element.383), channel_id=1, source_target_pairs={{0,32},{32,64},{64,96},{96,128},{128,160},{160,192},{192,224},{224... | collective-permute-start | bytes 393224 | tf_op jit(solution)/shard_map/while/body/eval_jaxpr/ppermute | solution.py:18
  214.7 11.4 %collective-permute-start.1 = (bf16[128,512]{0,1:T(8,128)(2,1)S(1)}, bf16[128,512]{0,1:T(8,128)(2,1)S(1)}, u32[]{:S(2)}, u32[]{:S(2)}) collective-permute-start(bf16[128,512]{0,1:T(8,128)(2,1)S(1)} %get-tuple-element.384), channel_id=1, source_target_pairs={{0,32},{32,64},{64,96},{96,128},{128,160},{160,192},{192,224},{224... | collective-permute-start | bytes 393224 | tf_op jit(solution)/shard_map/while/body/eval_jaxpr/ppermute | solution.py:18
  226.8 11.1 %collective-permute-start = (bf16[128,512]{0,1:T(8,128)(2,1)S(1)}, bf16[128,512]{0,1:T(8,128)(2,1)S(1)}, u32[]{:S(2)}, u32[]{:S(2)}) collective-permute-start(bf16[128,512]{0,1:T(8,128)(2,1)S(1)} %get-tuple-element.383), channel_id=1, source_target_pairs={{0,32},{32,64},{64,96},{96,128},{128,160},{160,192},{192,224},{224... | collective-permute-start | bytes 393224 | tf_op jit(solution)/shard_map/while/body/eval_jaxpr/ppermute | solution.py:18
  228.7 11.1 %collective-permute-start.1 = (bf16[128,512]{0,1:T(8,128)(2,1)S(1)}, bf16[128,512]{0,1:T(8,128)(2,1)S(1)}, u32[]{:S(2)}, u32[]{:S(2)}) collective-permute-start(bf16[128,512]{0,1:T(8,128)(2,1)S(1)} %get-tuple-element.384), channel_id=1, source_target_pairs={{0,32},{32,64},{64,96},{96,128},{128,160},{160,192},{192,224},{224... | collective-permute-start | bytes 393224 | tf_op jit(solution)/shard_map/while/body/eval_jaxpr/ppermute | solution.py:18
  241.1 3.4 copy-start.2
  241.1 5.6 %copy-start.3 = (bf16[1,128,2]{1,2,0:T(2,128)(2,1)S(1)}, bf16[1,128,2]{1,2,0:T(2,128)(2,1)}, u32[]{:S(2)}) copy-start(bf16[1,128,2]{1,2,0:T(2,128)(2,1)} %param.17) | copy-start | bytes 1540
  344.2 57.8 %copy-start.1 = (f32[128,448]{0,1:T(8,128)S(1)}, f32[128,448]{0,1:T(8,128)}, u32[]{:S(2)}) copy-start(f32[128,448]{0,1:T(8,128)} %fusion.55) | copy-start | bytes 688132
Sparse Core Ops, SparseCore 0:
  10.1 118.4 all-gather.7
  130.7 132.3 all-gather.3
  265.2 131.2 all-gather.5
  405.6 105.6 reduce-scatter.1
where the time goes:
time: 522 us; the launch traced here: 520 us
  waiting for transfers between devices  258 us (49%)
  blocking collectives  117 us (22%)
  starting transfers between devices  75.9 us (15%)
  matrix products  32.9 us (6%)
  between operations  14.6 us (3%)
  local copies, waits for them, and re-layouts  13.6 us (3%)
  other arithmetic  6.85 us (1%)
    reduce_scatter x1, waiting for transfers between devices, on_device(): lax.psum_scatter((result + lax.dot_general(grad_up, up_panel, contract_la...  104 us
    ppermute x30, waiting for transfers between devices, from_behind(): lax.ppermute(shard, axis, [(i, (i + by) % length) for i in range(length)])  99.2 us
    ppermute x30, starting transfers between devices, from_behind(): lax.ppermute(shard, axis, [(i, (i + by) % length) for i in range(length)])  75.7 us
    all_gather x1, waiting for transfers between devices, on_device(): lax.all_gather(up_weight, 'fsdp', axis=0, tiled=True)  52.3 us
    unnamed x1, blocking collectives  41.1 us
    all_gather x1, blocking collectives, on_device(): lax.all_gather(slot_dy, 'ctx', axis=0, tiled=True)  26.3 us
    all_gather x1, blocking collectives, on_device(): every_doc = lax.all_gather(doc_ids, 'ctx', axis=1, tiled=True)[0]  25.9 us
    all_gather x1, blocking collectives, on_device(): lax.all_gather(slot_x, 'ctx', axis=0, tiled=True)  23.5 us
  transfers between devices with their start and end apart: 34, of which 32 were waited for; matrix products, arithmetic and copies ran while one was open for 8% of the time, Pallas kernels for 0%

commit v1 on v0

v1 whole, which is shorter than its diff:
```python
import jax
import jax.numpy as jnp
from jax import lax
from jax.experimental import pallas as pl
from jax.experimental.pallas import tpu as pltpu
from jax.sharding import Mesh
from jax.sharding import PartitionSpec as P

HEADS = 16
KV_HEADS = 4
HEAD_DIM = 128
CAP = 8
TOK = 128
D = 2048
DOCS = 8
EPS = 1e-05
LOG2E = 1.4426950408889634
QW = HEADS * HEAD_DIM // 2
KW = KV_HEADS * HEAD_DIM // 2
ROWS = TOK + 8
FAR = -(2.0**20)
PAY = 2 * D + 128
HALF = 256
F32, BF16 = jnp.float32, jnp.bfloat16
CHIPS = ("y", "xh")
PEERS = ("y", "xh", "xl")
CTX = ("y", "xh", "core")
FSDP = ("z", "xl")
NT = (((1,), (1,)), ((), ()))
TN = (((0,), (0,)), ((), ()))


def call(kernel, out_shape, *operands, flops=0, smem=0, **kw):
    nbytes = sum(o.size * o.dtype.itemsize for o in operands)
    nbytes += sum(o.size * o.dtype.itemsize for o in jax.tree.leaves(out_shape))
    vmem = pl.BlockSpec(memory_space=pltpu.VMEM)
    specs = [pl.BlockSpec(memory_space=pltpu.SMEM)] * smem + [vmem] * (len(operands) - smem)
    return pl.pallas_call(
        kernel,
        out_shape=out_shape,
        in_specs=specs,
        out_specs=jax.tree.map(lambda _: vmem, out_shape),
        cost_estimate=pl.CostEstimate(flops=flops, bytes_accessed=nbytes, transcendentals=0),
        **kw,
    )(*operands)


def pack_weights(gate_ref, up_ref, down_ref, out_ref):
    rows = gate_ref.shape[0]
    ff = gate_ref.shape[1]
    rest = ff - HALF
    eye = lax.broadcasted_iota(jnp.int32, (rows, rows), 0) == lax.broadcasted_iota(
        jnp.int32, (rows, rows), 1
    )
    down = lax.dot_general(
        eye.astype(BF16), down_ref[...], NT, preferred_element_type=F32
    ).astype(BF16)
    for i, full in enumerate((gate_ref[...], up_ref[...], down)):
        here = slice(i * rows, (i + 1) * rows)
        out_ref[0, here, :] = full[:, :HALF]
        out_ref[1, here, :] = jnp.concatenate(
            [full[:, HALF:], jnp.zeros((rows, HALF - rest), BF16)], axis=1
        )


def pack_heads(q_ref, k_ref, v_ref, doc_ref, out_ref):
    docs = jnp.broadcast_to(doc_ref[...].astype(F32), (8, TOK)).astype(BF16)
    for c in range(2):
        out_ref[c, :TOK, :QW] = q_ref[0, :, c * QW : (c + 1) * QW]
        out_ref[c, :TOK, QW : QW + KW] = k_ref[0, :, c * KW : (c + 1) * KW]
        out_ref[c, :TOK, QW + KW :] = v_ref[0, :, c * KW : (c + 1) * KW]
        out_ref[c, TOK:, :] = jnp.zeros((8, QW + 2 * KW), BF16)
        out_ref[c, TOK:, QW : QW + TOK] = docs


def attend(base_ref, q_ref, kv_ref, out_ref, k_aug, v_aug):
    length = k_aug.shape[1]
    docs = kv_ref[:, TOK:, :TOK].astype(F32)
    lane = lax.broadcasted_iota(jnp.int32, (1, 128), 1)
    first = jnp.zeros((1, 128), F32)
    after = jnp.where(lane < DOCS, float(length), 0.0)
    for d in range(1, DOCS):
        below = jnp.sum(jnp.where(docs < float(d), 1.0, 0.0), axis=0)
        count = jnp.sum(below[:1], axis=1, keepdims=True)
        first = jnp.where(lane == d, count, first)
        after = jnp.where(lane == d - 1, count, after)
    spot = lax.broadcasted_iota(jnp.int32, (length, 128), 0).astype(F32)
    inside = (spot >= first) & (spot < after)
    k_doc = jnp.where(inside, 0.0, FAR).astype(BF16)
    for g in range(2):
        here = slice(g * HEAD_DIM, (g + 1) * HEAD_DIM)
        there = slice(KW + g * HEAD_DIM, KW + (g + 1) * HEAD_DIM)
        k_aug[g, :, :HEAD_DIM] = kv_ref[:, :TOK, here].reshape(length, HEAD_DIM)
        k_aug[g, :, HEAD_DIM:] = k_doc
        v_aug[g, :, :HEAD_DIM] = kv_ref[:, :TOK, there].reshape(length, HEAD_DIM)
        v_aug[g, :, HEAD_DIM:] = jnp.ones((length, HEAD_DIM), BF16)
    mine = (lax.broadcasted_iota(jnp.int32, (2 * TOK, 128), 0) + base_ref[0, 0]).astype(F32)
    q_doc = jnp.where((mine >= first) & (mine < after), 1.0, 0.0).astype(BF16)
    factor = HEAD_DIM**-0.5 * LOG2E
    for h in range(HEADS // 2):
        g = h // (HEADS // KV_HEADS)
        here = slice(h * HEAD_DIM, (h + 1) * HEAD_DIM)
        q = q_ref[:, :TOK, here].reshape(2 * TOK, HEAD_DIM)
        q = jnp.concatenate([q, q_doc], axis=1)
        scores = lax.dot_general(q, k_aug[g], NT, preferred_element_type=F32)
        top = jnp.max(scores, axis=1, keepdims=True)
        probs = jnp.exp2((scores - top) * factor).astype(BF16)
        mixed = jnp.dot(probs, v_aug[g], preferred_element_type=F32)
        mixed = (mixed[:, :HEAD_DIM] / mixed[:, HEAD_DIM:]).astype(BF16)
        out_ref[:, :, here] = mixed.reshape(2, TOK, HEAD_DIM)


def selection(route_ref, width):
    chosen = route_ref[0] == 0
    routed = jnp.max(jnp.where(chosen, 1.0, 0.0), axis=1, keepdims=True)
    rows = lax.broadcasted_iota(jnp.int32, (TOK, TOK), 0)
    cols = lax.broadcasted_iota(jnp.int32, (TOK, TOK), 1)
    upto = (cols <= rows).astype(F32).astype(BF16)
    wide = jnp.broadcast_to(routed, (TOK, 128)).astype(BF16)
    slot = jnp.dot(upto, wide, preferred_element_type=F32) - 1.0
    lane = cols.astype(F32)
    hit = (slot == lane) & (lane < float(CAP))
    if width == 2:
        hit = hit | ((slot + float(CAP) == lane) & (slot < float(CAP)))
    return jnp.where(hit & (routed > 0.5), 1.0, 0.0), chosen


def normalized(attn):
    square = jnp.mean(attn * attn, axis=1, keepdims=True)
    inverse = lax.rsqrt(square + EPS)
    return inverse, attn * inverse


def send_slots(mixed_ref, route_ref, rw_ref, cot_ref, attn_ref, pay_ref):
    for c in range(2):
        attn_ref[0, :, c * QW : (c + 1) * QW] = mixed_ref[c]
    _, scaled = normalized(attn_ref[0].astype(F32))
    select, chosen = selection(route_ref, 1)
    select = select.astype(BF16)
    weight = jnp.sum(jnp.where(chosen, rw_ref[0].astype(F32), 0.0), axis=1, keepdims=True)
    weight = jnp.broadcast_to(weight, (TOK, 128)).astype(BF16)

    def take(rows):
        got = lax.dot_general(select, rows, TN, preferred_element_type=F32)
        return got[:CAP].astype(BF16)

    x, dy, w = take(scaled.astype(BF16)), take(cot_ref[0]), take(weight)
    for i in range(pay_ref.shape[0] // CAP):
        here = slice(i * CAP, (i + 1) * CAP)
        pay_ref[here, :D] = x
        pay_ref[here, D : 2 * D] = dy
        pay_ref[here, 2 * D :] = w


def expert(own_ref, other_ref, w_ref, own_out, other_out):
    def panel(i):
        return w_ref[:, i * 64 : (i + 1) * 64, :].reshape(D, HALF)

    gate_w, up_w, down_w = panel(0), panel(1), panel(2)
    for ref, out in ((own_ref, own_out), (other_ref, other_out)):
        x, dy = ref[:, :D], ref[:, D : 2 * D]
        gate = jnp.dot(x, gate_w, preferred_element_type=F32)
        up = jnp.dot(x, up_w, preferred_element_type=F32)
        back = jnp.dot(dy, down_w, preferred_element_type=F32)
        back = back * ref[:, 2 * D : 2 * D + 1].astype(F32)
        sg = jax.nn.sigmoid(gate)
        grad_gate = (back * up * sg * (1.0 + gate * (1.0 - sg))).astype(BF16)
        grad_up = (back * gate * sg).astype(BF16)
        part = lax.dot_general(grad_gate, gate_w, NT, preferred_element_type=F32)
        part = part + lax.dot_general(grad_up, up_w, NT, preferred_element_type=F32)
        out[...] = part.astype(out.dtype)


def finish(attn_ref, route_ref, part_ref, out_ref):
    total = part_ref[0].astype(F32)
    for i in range(1, part_ref.shape[0]):
        total = total + part_ref[i].astype(F32)
    high = total.astype(BF16)
    low = (total - high.astype(F32)).astype(BF16)
    inverse, scaled = normalized(attn_ref[0].astype(F32))
    select, _ = selection(route_ref, 2)
    pair = jnp.concatenate([high.astype(F32), low.astype(F32)], axis=0).astype(BF16)
    d_norm = jnp.dot(
        select[:, : 2 * CAP].astype(BF16), pair, preferred_element_type=F32
    )
    mean = jnp.mean(d_norm * scaled, axis=1, keepdims=True)
    out_ref[0] = (inverse * (d_norm - scaled * mean)).astype(BF16)


def all_to_all(x, axes):
    return lax.all_to_all(x, axes, 0, 0, tiled=True)


def swap_cores(x):
    return lax.ppermute(x, "core", [(0, 1), (1, 0)])


def on_device(q, k, v, doc_ids, routes, route_weight, cotangent, gate_w, up_w, down_w):
    shape = jax.ShapeDtypeStruct
    rows = gate_w.shape[0]
    halves = call(pack_weights, shape((2, 3 * rows, HALF), BF16), gate_w, up_w, down_w)
    halves = all_to_all(halves.reshape(6 * rows, HALF), "xl")
    panels = lax.all_gather(halves, "z", axis=0, tiled=True)
    panels = panels.reshape(-1, 3 * rows, HALF)

    width = QW + 2 * KW
    packed = call(pack_heads, shape((2, ROWS, width), BF16), q, k, v, doc_ids)
    packed = all_to_all(packed.reshape(2 * ROWS, width), "core")
    chips = lax.axis_size(CHIPS)
    kv = jnp.broadcast_to(packed[None, :, QW:], (chips, 2 * ROWS, 2 * KW))
    kv = all_to_all(kv.reshape(chips * 2 * ROWS, 2 * KW), CHIPS).reshape(-1, ROWS, 2 * KW)
    length = kv.shape[0] * TOK
    base = (lax.axis_index(CHIPS) * (2 * TOK)).astype(jnp.int32).reshape(1, 1)
    mixed = call(
        attend,
        shape((2, TOK, QW), BF16),
        base,
        packed.reshape(2, ROWS, width),
        kv,
        smem=1,
        flops=16 * TOK * length * QW,
        scratch_shapes=[pltpu.VMEM((2, length, 2 * HEAD_DIM), BF16)] * 2,
    )
    mixed = all_to_all(mixed.reshape(2 * TOK, QW), "core").reshape(2, TOK, QW)
    peers = lax.axis_size(PEERS)
    attn, pay = call(
        send_slots,
        (shape((1, TOK, D), BF16), shape((peers * CAP, PAY), BF16)),
        mixed,
        routes,
        route_weight,
        cotangent,
    )
    own = all_to_all(pay, PEERS)
    other = swap_cores(own)
    own_part, other_part = call(
        expert,
        (shape((peers * CAP, D), F32), shape((peers * CAP, D), BF16)),
        own,
        other,
        panels,
        flops=20 * peers * CAP * D * HALF,
    )
    part = (own_part + swap_cores(other_part).astype(F32)).astype(BF16)
    part = all_to_all(part, PEERS).reshape(peers, CAP, D)
    d_input = call(finish, shape((1, TOK, D), BF16), attn, routes, part)
    return attn, d_input


def solution(mesh):
    fine = Mesh(mesh.devices.reshape(4, 2, 2, 16, 2), ("y", "xh", "core", "z", "xl"))
    return jax.shard_map(
        on_device,
        mesh=fine,
        in_specs=(
            P(FSDP, CTX, None),
            P(FSDP, CTX, None),
            P(FSDP, CTX, None),
            P(FSDP, CTX),
            P(FSDP, CTX, None),
            P(FSDP, CTX, None),
            P(FSDP, CTX, None),
            P(FSDP, CTX),
            P(FSDP, CTX),
            P(CTX, FSDP),
        ),
        out_specs=(P(FSDP, CTX, None), P(FSDP, CTX, None)),
        check_vma=False,
    )
```

time: 522 us -> 152 us (0.29)
  waiting for transfers between devices: 258 us -> 32.1 us
  starting transfers between devices: 75.9 us -> 9.58 us
  blocking collectives: 117 us -> 62.8 us
  matrix products: 32.9 us -> 0 us
  Pallas kernels: 0 us -> 24.3 us
  local copies, waits for them, and re-layouts: 13.6 us -> 7.12 us
  other arithmetic: 6.85 us -> 1.33 us
    reduce_scatter x1 -> x0, waiting for transfers between devices: 104 us -> none  [on_device(): lax.psum_scatter((result + lax.dot_general(grad_up, up_panel, contract_la...]
    ppermute x30 -> x2, waiting for transfers between devices: 99.2 us -> 4.04 us  [swap_cores(): return lax.ppermute(x, 'core', [(0, 1), (1, 0)])]
    all_gather x3 -> x0, blocking collectives: 75.7 us -> none  [the longest x1 26.3 us: on_device(): lax.all_gather(slot_dy, 'ctx', axis=0, tiled=True)]
    ppermute x30 -> x2, starting transfers between devices: 75.7 us -> 5.8 us  [swap_cores(): return lax.ppermute(x, 'core', [(0, 1), (1, 0)])]
    all_to_all x0 -> x5, blocking collectives: none -> 62.8 us  [all_to_all(): return lax.all_to_all(x, axes, 0, 0, tiled=True)]
    all_gather x3 -> x1, waiting for transfers between devices: 52.3 us -> 0.01 us  [on_device(): panels = lax.all_gather(halves, 'z', axis=0, tiled=True)]
    unnamed x1 -> x0, blocking collectives: 41.1 us -> none
    dot_general x40 -> x0, matrix products: 32.9 us -> none  [the longest x16 10.6 us: attend_block(): jnp.einsum('grij,jgd->grid', probabilities, value_heads, preferred_elemen...]
  transfers between devices with their start and end apart: 34 -> 4, of which waited for: 32 -> 3; matrix products, arithmetic and copies ran while one was open for 8% -> 2% of each run, Pallas kernels for 0% -> 9%
where the time goes in v1:
time: 152 us; the launch traced here: 151 us
  blocking collectives  62.8 us (41%)
  waiting for transfers between devices  32.1 us (21%)
  Pallas kernels  24.3 us (16%)
  between operations  14.1 us (9%)
  starting transfers between devices  9.58 us (6%)
  local copies, waits for them, and re-layouts  7.12 us (5%)
    all_to_all x5, blocking collectives, all_to_all(): return lax.all_to_all(x, axes, 0, 0, tiled=True)  62.8 us
    all_to_all x1, waiting for transfers between devices, all_to_all(): return lax.all_to_all(x, axes, 0, 0, tiled=True)  28 us
    pallas_call x6, Pallas kernels, call(): pl.pallas_call(kernel, out_shape=out_shape, in_specs=specs, out_specs=jax...  24.3 us
    ppermute x2, starting transfers between devices, swap_cores(): return lax.ppermute(x, 'core', [(0, 1), (1, 0)])  5.8 us
    unnamed x15, local copies, waits for them, and re-layouts  5.46 us
    ppermute x2, waiting for transfers between devices, swap_cores(): return lax.ppermute(x, 'core', [(0, 1), (1, 0)])  4.04 us
    all_to_all x1, starting transfers between devices, all_to_all(): return lax.all_to_all(x, axes, 0, 0, tiled=True)  3.74 us
  transfers between devices with their start and end apart: 4, of which 3 were waited for; matrix products, arithmetic and copies ran while one was open for 2% of the time, Pallas kernels for 9%

profile of v1, /device:TPU:1, one launch (start us, length us, event | category | flops | bytes accessed | tf_op | source)
XLA Modules:
  0.0 151.3 jit_solution(14180104260785640376)
XLA Ops:
  7.2 0.0 all-gather.2.cloned.1.call-start
  7.2 1.6 %copy.14.down_ref = bf16[448,64]{1,0:T(8,128)(2,1)} copy(bf16[448,64]{0,1:T(8,128)(2,1)} %param.19) | data formatting | bytes 114688 | tf_op args[9]
  8.8 1.8 %shard_map.116 = bf16[2,192,256]{2,1,0:T(8,128)(2,1)} custom-call(bf16[64,448]{1,0:T(8,128)(2,1)} %gate_ref.1, bf16[64,448]{1,0:T(8,128)(2,1)} %up_ref.1, bf16[448,64]{1,0:T(8,128)(2,1)} %copy.14.down_ref), custom_call_target="tpu_custom_call" | custom-call | bytes 368640 | tf_op jit(solution)/shard_map/pallas_call | solution.py:38
  10.6 8.4 %all_to_all.50 = bf16[2,192,256]{2,1,0:T(8,128)(2,1)} all-to-all(bf16[2,192,256]{2,1,0:T(8,128)(2,1)} %shard_map.116), channel_id=1, replica_groups=mesh['y'=4,'xh'=2,'core'=2,'z'=16,'xl'=2] {'xl'}, dimensions={0} | all-to-all | bytes 393216 | tf_op jit(solution)/shard_map/all_to_all | solution.py:191
  19.1 0.0 all-gather.2.cloned.1.call-update
  19.1 2.1 %shard_map.113 = bf16[2,136,1536]{2,1,0:T(8,128)(2,1)} custom-call(bf16[1,128,2048]{2,1,0:T(8,128)(2,1)} %q_ref.1, bf16[1,128,512]{2,1,0:T(8,128)(2,1)} %k_ref.1, bf16[1,128,512]{2,1,0:T(8,128)(2,1)} %v_ref.1, s32[1,128]{1,0:T(1,128)} %doc_ref.1), custom_call_target="tpu_custom_call" | custom-call | bytes 1622528 | tf_op jit(solution)/shard_map/pallas_call | solution.py:38
  21.2 12.5 %all_to_all.51.q_ref = bf16[2,136,1536]{2,1,0:T(8,128)(2,1)S(1)} all-to-all(bf16[2,136,1536]{2,1,0:T(8,128)(2,1)} %shard_map.113), channel_id=1, replica_groups=mesh['y'=4,'xh'=2,'core'=2,'z'=16,'xl'=2] {'core'}, dimensions={0} | all-to-all | bytes 1671168 | tf_op jit(solution)/shard_map/all_to_all | solution.py:191
  33.7 0.0 copy-start.2
  33.7 1.6 %broadcast_in_dim.2 = bf16[8,272,512]{2,1,0:T(8,128)(2,1)} broadcast(bf16[272,512]{1,0:T(8,128)(2,1)S(1)} %slice.4), dimensions={1,2} | broadcast | bytes 2506752 | tf_op jit(solution)/shard_map/broadcast_in_dim | solution.py:210
  35.4 0.0 copy-start.4
  35.4 0.0 copy-start.5
  35.4 0.0 copy-done.2
  35.4 3.7 %all-to-all-start.1 = ((bf16[8,272,512]{2,1,0:T(8,128)(2,1)}), bf16[8,272,512]{2,1,0:T(8,128)(2,1)S(1)}, u32[]{:S(2)}, u32[]{:S(2)}) async-start(bf16[8,272,512]{2,1,0:T(8,128)(2,1)} %broadcast_in_dim.2), calls=%async_computation.1 | async-start | bytes 4456448 | tf_op jit(solution)/shard_map/all_to_all | solution.py:191
  39.2 0.0 copy-done.4
  39.2 0.7 copy.12.route_ref
  39.9 0.0 copy-done.5
  39.9 0.7 copy.13.rw_ref
  40.6 28.0 %all-to-all-done.1 = bf16[8,272,512]{2,1,0:T(8,128)(2,1)S(1)} async-done(((bf16[8,272,512]{2,1,0:T(8,128)(2,1)}), bf16[8,272,512]{2,1,0:T(8,128)(2,1)S(1)}, u32[]{:S(2)}, u32[]{:S(2)}) %all-to-all-start.1) | async-done | bytes 2228256 | tf_op jit(solution)/shard_map/all_to_all | solution.py:191
  68.7 0.0 copy-start.1
  68.7 1.4 copy-done.1
  70.1 8.6 %shard_map.114 = bf16[2,128,1024]{2,1,0:T(8,128)(2,1)} custom-call(s32[1,1]{1,0:T(1,128)} %bitcast.base_ref, bf16[2,136,1536]{2,1,0:T(8,128)(2,1)} %copy-done.2, bf16[16,136,512]{2,1,0:T(8,128)(2,1)} %bitcast.12), custom_call_target="tpu_custom_call" | custom-call | flops 4294967296 | bytes 3588100 | tf_op jit(solution)/shard_map/pallas_call | solution.py:38
  78.6 7.0 %all_to_all.52.mixed_ref = bf16[2,128,1024]{2,1,0:T(8,128)(2,1)} all-to-all(bf16[2,128,1024]{2,1,0:T(8,128)(2,1)} %shard_map.114), channel_id=1, replica_groups=mesh['y'=4,'xh'=2,'core'=2,'z'=16,'xl'=2] {'core'}, dimensions={0} | all-to-all | bytes 1048576 | tf_op jit(solution)/shard_map/all_to_all | solution.py:191
  85.6 3.0 %shard_map.115 = (bf16[1,128,2048]{2,1,0:T(8,128)(2,1)}, bf16[128,4224]{1,0:T(8,128)(2,1)}) custom-call(bf16[2,128,1024]{2,1,0:T(8,128)(2,1)} %all_to_all.52.mixed_ref, s32[1,128,2]{2,1,0:T(8,128)} %copy.12.route_ref, bf16[1,128,2]{2,1,0:T(8,128)(2,1)} %copy.13.rw_ref, bf16[1,128,2048]{2,1,0:T(8,128)(2,1)} %cot_ref.1), custom_call_target="tpu_custom_call" | custom-call | bytes 2655744 | tf_op jit(solution)/shard_map/pallas_call | solution.py:38
  88.6 20.6 %all_to_all.53 = bf16[16,8,4224]{2,1,0:T(8,128)(2,1)S(1)} all-to-all(bf16[16,8,4224]{2,1,0:T(8,128)(2,1)} %bitcast.14), channel_id=1, replica_groups=mesh['y'=4,'xh'=2,'core'=2,'z'=16,'xl'=2] {'y','xh','xl'}, dimensions={0} | all-to-all | bytes 2162688 | tf_op jit(solution)/shard_map/all_to_all | solution.py:191
  109.2 0.0 copy-start
  109.2 3.5 %collective-permute-start = (bf16[128,4224]{1,0:T(8,128)(2,1)S(1)}, bf16[128,4224]{1,0:T(8,128)(2,1)S(1)}, u32[]{:S(2)}, u32[]{:S(2)}) collective-permute-start(bf16[128,4224]{1,0:T(8,128)(2,1)S(1)} %bitcast.9), channel_id=1, source_target_pairs={{0,32},{32,0},{1,33},{33,1},{2,34},{34,2},{3,35},{35,3},{4,36},{36... | collective-permute-start | bytes 3244040 | tf_op jit(solution)/shard_map/ppermute | solution.py:195
  112.7 2.3 %collective-permute-done.other_ref = bf16[128,4224]{1,0:T(8,128)(2,1)S(1)} collective-permute-done((bf16[128,4224]{1,0:T(8,128)(2,1)S(1)}, bf16[128,4224]{1,0:T(8,128)(2,1)S(1)}, u32[]{:S(2)}, u32[]{:S(2)}) %collective-permute-start) | collective-permute-done | bytes 1081376 | tf_op jit(solution)/shard_map/ppermute | solution.py:195
  115.1 0.0 copy-start.3
  115.1 0.0 all-gather.2.cloned.1.call-done
  115.1 0.0 copy-done
  115.1 1.0 copy-done.3
  116.0 6.0 %shard_map.117 = (f32[128,2048]{1,0:T(8,128)}, bf16[128,2048]{1,0:T(8,128)(2,1)}) custom-call(bf16[128,4224]{1,0:T(8,128)(2,1)} %bitcast.10, bf16[128,4224]{1,0:T(8,128)(2,1)} %copy-done.3, bf16[32,192,256]{2,1,0:T(8,128)(2,1)} %bitcast.11), custom_call_target="tpu_custom_call" | custom-call | flops 1342177280 | bytes 6881280 | tf_op jit(solution)/shard_map/pallas_call | solution.py:38
  122.1 2.3 %collective-permute-start.1 = (bf16[128,2048]{1,0:T(8,128)(2,1)}, bf16[128,2048]{1,0:T(8,128)(2,1)S(1)}, u32[]{:S(2)}, u32[]{:S(2)}) collective-permute-start(bf16[128,2048]{1,0:T(8,128)(2,1)} %get-tuple-element.9), channel_id=1, source_target_pairs={{0,32},{32,0},{1,33},{33,1},{2,34},{34,2},{3,35},{35,3},{4,36},{36... | collective-permute-start | bytes 1572872 | tf_op jit(solution)/shard_map/ppermute | solution.py:195
  124.3 1.7 %collective-permute-done.1 = bf16[128,2048]{1,0:T(8,128)(2,1)S(1)} collective-permute-done((bf16[128,2048]{1,0:T(8,128)(2,1)}, bf16[128,2048]{1,0:T(8,128)(2,1)S(1)}, u32[]{:S(2)}, u32[]{:S(2)}) %collective-permute-start.1) | collective-permute-done | bytes 524320 | tf_op jit(solution)/shard_map/ppermute | solution.py:195
  126.1 1.3 fusion
  127.4 14.2 %all_to_all.54.part_ref = bf16[16,8,2048]{2,1,0:T(8,128)(2,1)} all-to-all(bf16[16,8,2048]{2,1,0:T(8,128)(2,1)S(1)} %fusion), channel_id=1, replica_groups=mesh['y'=4,'xh'=2,'core'=2,'z'=16,'xl'=2] {'y','xh','xl'}, dimensions={0} | all-to-all | bytes 1048576 | tf_op jit(solution)/shard_map/all_to_all | solution.py:191
  141.7 2.8 %shard_map.118 = bf16[1,128,2048]{2,1,0:T(8,128)(2,1)} custom-call(bf16[1,128,2048]{2,1,0:T(8,128)(2,1)} %get-tuple-element.4.attn_ref, s32[1,128,2]{2,1,0:T(8,128)} %copy.12.route_ref, bf16[16,8,2048]{2,1,0:T(8,128)(2,1)} %all_to_all.54.part_ref), custom_call_target="tpu_custom_call" | custom-call | bytes 1573888 | tf_op jit(solution)/shard_map/pallas_call | solution.py:38
  (1 shorter events, 0.0 us)
Async XLA Ops:
  7.2 107.9 %all-gather.2.cloned.1.call-start = ((), (), s32[]{:S(2)}) async-start(), calls=%async_computation.6 | async-start | bytes 3342336 | tf_op jit(solution)/shard_map/all_gather | solution.py:203
  33.7 1.7 %copy-start.2 = (bf16[2,136,1536]{2,1,0:T(8,128)(2,1)}, bf16[2,136,1536]{2,1,0:T(8,128)(2,1)S(1)}, u32[]{:S(2)}) copy-start(bf16[2,136,1536]{2,1,0:T(8,128)(2,1)S(1)} %all_to_all.51.q_ref) | copy-start | bytes 2506756
  35.4 3.8 %copy-start.4 = (s32[1,128,2]{1,2,0:T(2,128)S(1)}, s32[1,128,2]{1,2,0:T(2,128)}, u32[]{:S(2)}) copy-start(s32[1,128,2]{1,2,0:T(2,128)} %param.14) | copy-start | bytes 3076
  35.4 4.5 %copy-start.5 = (bf16[1,128,2]{1,2,0:T(2,128)(2,1)S(1)}, bf16[1,128,2]{1,2,0:T(2,128)(2,1)}, u32[]{:S(2)}) copy-start(bf16[1,128,2]{1,2,0:T(2,128)(2,1)} %param.15) | copy-start | bytes 1540
  35.4 33.3 %all-to-all-start.1 = ((bf16[8,272,512]{2,1,0:T(8,128)(2,1)}), bf16[8,272,512]{2,1,0:T(8,128)(2,1)S(1)}, u32[]{:S(2)}, u32[]{:S(2)}) async-start(bf16[8,272,512]{2,1,0:T(8,128)(2,1)} %broadcast_in_dim.2), calls=%async_computation.1 | async-start | bytes 4456448 | tf_op jit(solution)/shard_map/all_to_all | solution.py:191
  68.7 1.4 copy-start.1
  109.2 5.9 %copy-start = (bf16[16,8,4224]{2,1,0:T(8,128)(2,1)}, bf16[16,8,4224]{2,1,0:T(8,128)(2,1)S(1)}, u32[]{:S(2)}) copy-start(bf16[16,8,4224]{2,1,0:T(8,128)(2,1)S(1)} %all_to_all.53) | copy-start | bytes 3244036
  109.2 5.9 %collective-permute-start = (bf16[128,4224]{1,0:T(8,128)(2,1)S(1)}, bf16[128,4224]{1,0:T(8,128)(2,1)S(1)}, u32[]{:S(2)}, u32[]{:S(2)}) collective-permute-start(bf16[128,4224]{1,0:T(8,128)(2,1)S(1)} %bitcast.9), channel_id=1, source_target_pairs={{0,32},{32,0},{1,33},{33,1},{2,34},{34,2},{3,35},{35,3},{4,36},{36... | collective-permute-start | bytes 3244040 | tf_op jit(solution)/shard_map/ppermute | solution.py:195
  115.1 1.0 copy-start.3
  122.1 4.0 %collective-permute-start.1 = (bf16[128,2048]{1,0:T(8,128)(2,1)}, bf16[128,2048]{1,0:T(8,128)(2,1)S(1)}, u32[]{:S(2)}, u32[]{:S(2)}) collective-permute-start(bf16[128,2048]{1,0:T(8,128)(2,1)} %get-tuple-element.9), channel_id=1, source_target_pairs={{0,32},{32,0},{1,33},{33,1},{2,34},{34,2},{3,35},{35,3},{4,36},{36... | collective-permute-start | bytes 1572872 | tf_op jit(solution)/shard_map/ppermute | solution.py:195
Sparse Core Ops, SparseCore 0:
  19.2 72.3 all-gather.1

commit v2 on v1

v2 whole, which is shorter than its diff:
```python
import jax
import jax.numpy as jnp
from jax import lax
from jax.experimental import pallas as pl
from jax.experimental.pallas import tpu as pltpu
from jax.sharding import Mesh
from jax.sharding import PartitionSpec as P

HEADS = 16
KV_HEADS = 4
HEAD_DIM = 128
CAP = 8
TOK = 128
D = 2048
DOCS = 8
EPS = 1e-05
LOG2E = 1.4426950408889634
QW = HEADS * HEAD_DIM // 2
KW = KV_HEADS * HEAD_DIM // 2
FAR = -(2.0**20)
HALF = 256
F32, BF16 = jnp.float32, jnp.bfloat16
CHIPS = ("y", "xh")
PEERS = ("y", "xh", "xl")
CTX = ("y", "xh", "core")
FSDP = ("z", "xl")
NT = (((1,), (1,)), ((), ()))
TN = (((0,), (0,)), ((), ()))


def call(kernel, out_shape, *operands, flops=0, smem=0, hbm=0, **kw):
    nbytes = sum(o.size * o.dtype.itemsize for o in operands)
    nbytes += sum(o.size * o.dtype.itemsize for o in jax.tree.leaves(out_shape))
    vmem = pl.BlockSpec(memory_space=pltpu.VMEM)
    specs = [pl.BlockSpec(memory_space=pltpu.SMEM)] * smem
    specs += [vmem] * (len(operands) - smem - hbm)
    specs += [pl.BlockSpec(memory_space=pl.ANY)] * hbm
    return pl.pallas_call(
        kernel,
        out_shape=out_shape,
        in_specs=specs,
        out_specs=jax.tree.map(lambda _: vmem, out_shape),
        cost_estimate=pl.CostEstimate(flops=flops, bytes_accessed=nbytes, transcendentals=0),
        **kw,
    )(*operands)


def pack_weights(side_ref, gate_ref, up_ref, down_ref, keep_ref, send_ref):
    rows = gate_ref.shape[0]
    rest = gate_ref.shape[1] - HALF

    def write(low_ref, high_ref):
        for i, ref in enumerate((gate_ref, up_ref, down_ref)):
            here = slice(i * rows, (i + 1) * rows)
            low_ref[here, :] = ref[:, :HALF]
            high_ref[here, :] = jnp.concatenate(
                [ref[:, HALF:], jnp.zeros((rows, HALF - rest), BF16)], axis=1
            )

    @pl.when(side_ref[0, 0] == 0)
    def _():
        write(keep_ref, send_ref)

    @pl.when(side_ref[0, 0] != 0)
    def _():
        write(send_ref, keep_ref)


def pack_heads(core_ref, q_ref, k_ref, v_ref, doc_ref, keep_ref, send_ref):
    docs = jnp.broadcast_to(doc_ref[...].astype(F32), (8, TOK)).astype(BF16)
    core = core_ref[0, 0]
    for side, out_ref in ((core, keep_ref), (1 - core, send_ref)):
        row = 0
        for ref, width in ((q_ref, QW), (k_ref, KW), (v_ref, KW)):
            for h in range(width // HEAD_DIM):
                start = pl.multiple_of(side * width + h * HEAD_DIM, HEAD_DIM)
                out_ref[row : row + TOK, :] = ref[0, :, pl.ds(start, HEAD_DIM)]
                row += TOK
        out_ref[row:, :] = docs


def attend(base_ref, own_ref, other_ref, kv_ref, keep_ref, send_ref, k_aug, v_aug):
    length = k_aug.shape[1]
    heads = KW // HEAD_DIM
    docs = kv_ref[:, 2 * heads * TOK :, :].astype(F32)
    lane = lax.broadcasted_iota(jnp.int32, (1, 128), 1)
    first = jnp.zeros((1, 128), F32)
    after = jnp.where(lane < DOCS, float(length), 0.0)
    for d in range(1, DOCS):
        below = jnp.sum(jnp.where(docs < float(d), 1.0, 0.0), axis=0)
        count = jnp.sum(below[:1], axis=1, keepdims=True)
        first = jnp.where(lane == d, count, first)
        after = jnp.where(lane == d - 1, count, after)
    turn = base_ref[0, 1]
    spot = (lax.broadcasted_iota(jnp.int32, (length, 128), 0) ^ turn).astype(F32)
    inside = (spot >= first) & (spot < after)
    k_doc = jnp.where(inside, 0.0, FAR).astype(BF16)
    for g in range(heads):
        here = slice(g * TOK, (g + 1) * TOK)
        there = slice((heads + g) * TOK, (heads + g + 1) * TOK)
        k_aug[g, :, :HEAD_DIM] = kv_ref[:, here, :].reshape(length, HEAD_DIM)
        k_aug[g, :, HEAD_DIM:] = k_doc
        v_aug[g, :, :HEAD_DIM] = kv_ref[:, there, :].reshape(length, HEAD_DIM)
        v_aug[g, :, HEAD_DIM:] = jnp.ones((length, HEAD_DIM), BF16)
    mine = lax.broadcasted_iota(jnp.int32, (2 * TOK, 128), 0) ^ turn
    mine = (mine + base_ref[0, 0]).astype(F32)
    q_doc = jnp.where((mine >= first) & (mine < after), 1.0, 0.0).astype(BF16)
    factor = HEAD_DIM**-0.5 * LOG2E
    for h in range(HEADS // 2):
        g = h // (HEADS // KV_HEADS)
        here = slice(h * HEAD_DIM, (h + 1) * HEAD_DIM)
        q = jnp.concatenate([own_ref[h * TOK : (h + 1) * TOK], other_ref[h * TOK : (h + 1) * TOK]], axis=0)
        q = jnp.concatenate([q, q_doc], axis=1)
        scores = lax.dot_general(q, k_aug[g], NT, preferred_element_type=F32)
        top = jnp.max(scores, axis=1, keepdims=True)
        probs = jnp.exp2((scores - top) * factor).astype(BF16)
        mixed = jnp.dot(probs, v_aug[g], preferred_element_type=F32)
        mixed = (mixed[:, :HEAD_DIM] / mixed[:, HEAD_DIM:]).astype(BF16)
        keep_ref[:, here] = mixed[:TOK]
        send_ref[:, here] = mixed[TOK:]


def selection(route_ref, width):
    chosen = route_ref[0] == 0
    routed = jnp.max(jnp.where(chosen, 1.0, 0.0), axis=1, keepdims=True)
    rows = lax.broadcasted_iota(jnp.int32, (TOK, TOK), 0)
    cols = lax.broadcasted_iota(jnp.int32, (TOK, TOK), 1)
    upto = (cols <= rows).astype(F32).astype(BF16)
    wide = jnp.broadcast_to(routed, (TOK, 128)).astype(BF16)
    slot = jnp.dot(upto, wide, preferred_element_type=F32) - 1.0
    lane = cols.astype(F32)
    hit = (slot == lane) & (lane < float(CAP))
    if width == 2:
        hit = hit | ((slot + float(CAP) == lane) & (slot < float(CAP)))
    return jnp.where(hit & (routed > 0.5), 1.0, 0.0), chosen


def normalized(attn):
    square = jnp.mean(attn * attn, axis=1, keepdims=True)
    inverse = lax.rsqrt(square + EPS)
    return inverse, attn * inverse


def copies(rows, out_ref):
    for i in range(out_ref.shape[0] // CAP):
        out_ref[i * CAP : (i + 1) * CAP, :] = rows


def take(select, rows):
    got = lax.dot_general(select.astype(BF16), rows, TN, preferred_element_type=F32)
    return got[:CAP].astype(BF16)


def send_grads(route_ref, rw_ref, cot_ref, pay_ref):
    select, chosen = selection(route_ref, 1)
    weight = jnp.sum(jnp.where(chosen, rw_ref[0].astype(F32), 0.0), axis=1, keepdims=True)
    weight = jnp.broadcast_to(weight, (TOK, 128)).astype(BF16)
    copies(jnp.concatenate([take(select, cot_ref[0]), take(select, weight)], axis=1), pay_ref)


def send_slots(core_ref, own_ref, other_ref, route_ref, attn_ref, pay_ref):
    core = core_ref[0, 0]
    for side, ref in ((core, own_ref), (1 - core, other_ref)):
        attn_ref[0, :, pl.ds(pl.multiple_of(side * QW, QW), QW)] = ref[...]
    _, scaled = normalized(attn_ref[0].astype(F32))
    select, _ = selection(route_ref, 1)
    copies(take(select, scaled.astype(BF16)), pay_ref)


def expert(x_ref, x2_ref, dy_ref, dy2_ref, w_ref, own_out, other_out, panels, sems):
    depth = panels.shape[2]
    loads = [
        pltpu.make_async_copy(w_ref.at[:, pl.ds(i * depth, depth), :], panels.at[i], sems.at[i])
        for i in range(3)
    ]
    for i in (2, 0, 1):
        loads[i].start()

    def panel(i):
        return panels[i].reshape(D, HALF)

    dy = jnp.concatenate([dy_ref[...], dy2_ref[...]], axis=0)
    x = jnp.concatenate([x_ref[...], x2_ref[...]], axis=0)
    loads[2].wait()
    back = jnp.dot(dy[:, :D], panel(2), preferred_element_type=F32)
    back = back * dy[:, D : D + 1].astype(F32)
    loads[0].wait()
    gate = jnp.dot(x, panel(0), preferred_element_type=F32)
    loads[1].wait()
    up = jnp.dot(x, panel(1), preferred_element_type=F32)
    sg = jax.nn.sigmoid(gate)
    grad_gate = (back * up * sg * (1.0 + gate * (1.0 - sg))).astype(BF16)
    grad_up = (back * gate * sg).astype(BF16)
    part = lax.dot_general(grad_gate, panel(0), NT, preferred_element_type=F32)
    part = part + lax.dot_general(grad_up, panel(1), NT, preferred_element_type=F32)
    half = own_out.shape[0]
    own_out[...] = part[:half]
    other_out[...] = part[half:].astype(BF16)


def finish(attn_ref, route_ref, part_ref, out_ref):
    total = part_ref[0].astype(F32)
    for i in range(1, part_ref.shape[0]):
        total = total + part_ref[i].astype(F32)
    high = total.astype(BF16)
    low = (total - high.astype(F32)).astype(BF16)
    inverse, scaled = normalized(attn_ref[0].astype(F32))
    select, _ = selection(route_ref, 2)
    pair = jnp.concatenate([high.astype(F32), low.astype(F32)], axis=0).astype(BF16)
    d_norm = jnp.dot(
        select[:, : 2 * CAP].astype(BF16), pair, preferred_element_type=F32
    )
    mean = jnp.mean(d_norm * scaled, axis=1, keepdims=True)
    out_ref[0] = (inverse * (d_norm - scaled * mean)).astype(BF16)


def all_to_all(x, axes):
    return lax.all_to_all(x, axes, 0, 0, tiled=True)


def swap(x, axis):
    return lax.ppermute(x, axis, [(0, 1), (1, 0)])


def scalars(*values):
    return jnp.stack([jnp.asarray(v, jnp.int32) for v in values]).reshape(1, -1)


def on_device(q, k, v, doc_ids, routes, route_weight, cotangent, gate_w, up_w, down_w):
    shape = jax.ShapeDtypeStruct
    rows = gate_w.shape[0]
    side, core = lax.axis_index("xl"), lax.axis_index("core")
    peers, chips = lax.axis_size(PEERS), lax.axis_size(CHIPS)

    half = shape((3 * rows, HALF), BF16)
    keep_w, send_w = call(
        pack_weights, (half, half), scalars(side), gate_w, up_w, down_w.T, smem=1
    )
    got_w = swap(send_w, "xl")
    low = jnp.where(side == 0, keep_w, got_w)
    high = jnp.where(side == 0, got_w, keep_w)
    panels = lax.all_gather(jnp.concatenate([low, high]), "z", axis=0, tiled=True)
    panels = panels.reshape(-1, 3 * rows, HALF)

    block = QW + 2 * KW + 8
    packed = shape((block, HEAD_DIM), BF16)
    keep, send = call(
        pack_heads, (packed, packed), scalars(core), q, k, v, doc_ids, smem=1
    )
    got = swap(send, "core")
    kv = jnp.concatenate([keep[QW:], got[QW:]])
    kv = jnp.broadcast_to(kv[None], (chips, *kv.shape)).reshape(-1, HEAD_DIM)
    kv = all_to_all(kv, CHIPS).reshape(-1, block - QW, HEAD_DIM)
    length = kv.shape[0] * TOK

    dy = call(
        send_grads, shape((peers * CAP, D + 128), BF16), routes, route_weight, cotangent
    )
    dy, kv = lax.optimization_barrier((dy, kv))
    own_dy = all_to_all(dy, PEERS)
    other_dy = swap(own_dy, "core")

    mixed = shape((TOK, QW), BF16)
    keep_o, send_o = call(
        attend,
        (mixed, mixed),
        scalars(lax.axis_index(CHIPS) * (2 * TOK), core * TOK),
        keep,
        got,
        kv,
        smem=1,
        flops=16 * TOK * length * QW,
        scratch_shapes=[pltpu.VMEM((2, length, 2 * HEAD_DIM), BF16)] * 2,
    )
    attn, pay = call(
        send_slots,
        (shape((1, TOK, D), BF16), shape((peers * CAP, D), BF16)),
        scalars(core),
        keep_o,
        swap(send_o, "core"),
        routes,
        smem=1,
    )
    own_x = all_to_all(pay, PEERS)
    other_x = swap(own_x, "core")
    own_part, other_part = call(
        expert,
        (shape((peers * CAP, D), F32), shape((peers * CAP, D), BF16)),
        own_x,
        other_x,
        own_dy,
        other_dy,
        panels,
        hbm=1,
        flops=20 * peers * CAP * D * HALF,
        scratch_shapes=[
            pltpu.VMEM((3, panels.shape[0], rows, HALF), BF16),
            pltpu.SemaphoreType.DMA((3,)),
        ],
    )
    part = (own_part + swap(other_part, "core").astype(F32)).astype(BF16)
    part = all_to_all(part, PEERS).reshape(peers, CAP, D)
    d_input = call(finish, shape((1, TOK, D), BF16), attn, routes, part)
    return attn, d_input


def solution(mesh):
    fine = Mesh(mesh.devices.reshape(4, 2, 2, 16, 2), ("y", "xh", "core", "z", "xl"))
    return jax.shard_map(
        on_device,
        mesh=fine,
        in_specs=(
            P(FSDP, CTX, None),
            P(FSDP, CTX, None),
            P(FSDP, CTX, None),
            P(FSDP, CTX),
            P(FSDP, CTX, None),
            P(FSDP, CTX, None),
            P(FSDP, CTX, None),
            P(FSDP, CTX),
            P(FSDP, CTX),
            P(CTX, FSDP),
        ),
        out_specs=(P(FSDP, CTX, None), P(FSDP, CTX, None)),
        check_vma=False,
    )
```

time: 152 us -> 143 us (0.941)
  blocking collectives: 62.8 us -> 14.2 us
  starting transfers between devices: 9.58 us -> 39.1 us
  waiting for transfers between devices: 32.1 us -> 39.4 us
  other arithmetic: 1.33 us -> 3.62 us
  Pallas kernels: 24.3 us -> 26.2 us
  local copies, waits for them, and re-layouts: 7.12 us -> 5.52 us
    all_to_all x5 -> x1, blocking collectives: 62.8 us -> 14.2 us  [all_to_all(): return lax.all_to_all(x, axes, 0, 0, tiled=True)]
    ppermute x2 -> x6, starting transfers between devices: 5.8 us -> 24.9 us  [swap(): return lax.ppermute(x, axis, [(0, 1), (1, 0)])]
    all_to_all x1 -> x3, starting transfers between devices: 3.74 us -> 14.2 us  [all_to_all(): return lax.all_to_all(x, axes, 0, 0, tiled=True)]
    all_to_all x1 -> x3, waiting for transfers between devices: 28 us -> 32 us  [all_to_all(): return lax.all_to_all(x, axes, 0, 0, tiled=True)]
    ppermute x2 -> x6, waiting for transfers between devices: 4.04 us -> 7.39 us  [swap(): return lax.ppermute(x, axis, [(0, 1), (1, 0)])]
    unnamed x15 -> x20, local copies, waits for them, and re-layouts: 5.46 us -> 2.96 us
    pallas_call x6 -> x7, Pallas kernels: 24.3 us -> 26.2 us  [call(): pl.pallas_call(kernel, out_shape=out_shape, in_specs=specs, out_specs=jax...]
  transfers between devices with their start and end apart: 4 -> 10, of which waited for: 3 -> 7; matrix products, arithmetic and copies ran while one was open for 2% -> 3% of each run, Pallas kernels for 9% -> 11%
where the time goes in v2:
time: 143 us; the launch traced here: 142 us
  waiting for transfers between devices  39.4 us (28%)
  starting transfers between devices  39.1 us (27%)
  Pallas kernels  26.2 us (18%)
  blocking collectives  14.2 us (10%)
  between operations  14.2 us (10%)
  local copies, waits for them, and re-layouts  5.52 us (4%)
  other arithmetic  3.62 us (3%)
    all_to_all x3, waiting for transfers between devices, all_to_all(): return lax.all_to_all(x, axes, 0, 0, tiled=True)  32 us
    pallas_call x7, Pallas kernels, call(): pl.pallas_call(kernel, out_shape=out_shape, in_specs=specs, out_specs=jax...  26.2 us
    ppermute x6, starting transfers between devices, swap(): return lax.ppermute(x, axis, [(0, 1), (1, 0)])  24.9 us
    all_to_all x1, blocking collectives, all_to_all(): return lax.all_to_all(x, axes, 0, 0, tiled=True)  14.2 us
    all_to_all x3, starting transfers between devices, all_to_all(): return lax.all_to_all(x, axes, 0, 0, tiled=True)  14.2 us
    ppermute x6, waiting for transfers between devices, swap(): return lax.ppermute(x, axis, [(0, 1), (1, 0)])  7.39 us
    unnamed x20, local copies, waits for them, and re-layouts  2.96 us
  transfers between devices with their start and end apart: 10, of which 7 were waited for; matrix products, arithmetic and copies ran while one was open for 3% of the time, Pallas kernels for 11%

profile of v2, /device:TPU:1, one launch (start us, length us, event | category | flops | bytes accessed | tf_op | source)
XLA Modules:
  0.0 142.4 jit_solution(9970024277795402762)
XLA Ops:
  7.2 0.0 all-gather.2.cloned.1.call-start
  7.2 1.6 %shard_map.117 = (bf16[192,256]{1,0:T(8,128)(2,1)}, bf16[192,256]{1,0:T(8,128)(2,1)}) custom-call(s32[1,1]{1,0:T(1,128)} %bitcast.9.side_ref, bf16[64,448]{1,0:T(8,128)(2,1)} %gate_ref.1, bf16[64,448]{1,0:T(8,128)(2,1)} %up_ref.1, bf16[64,448]{1,0:T(8,128)(2,1)} %bitcast.23), custom_call_target="tpu_custom_call" | custom-call | bytes 368644 | tf_op jit(solution)/shard_map/pallas_call | solution.py:38
  8.8 3.9 %collective-permute-start.4 = (bf16[192,256]{1,0:T(8,128)(2,1)}, bf16[192,256]{1,0:T(8,128)(2,1)S(1)}, u32[]{:S(2)}, u32[]{:S(2)}) collective-permute-start(bf16[192,256]{1,0:T(8,128)(2,1)} %get-tuple-element.23), channel_id=1, source_target_pairs={{0,1},{1,0},{2,3},{3,2},{4,5},{5,4},{6,7},{7,6},{8,9},{9,8},{10,11... | collective-permute-start | bytes 294920 | tf_op jit(solution)/shard_map/ppermute | solution.py:222
  12.7 2.2 %collective-permute-done.4 = bf16[192,256]{1,0:T(8,128)(2,1)S(1)} collective-permute-done((bf16[192,256]{1,0:T(8,128)(2,1)}, bf16[192,256]{1,0:T(8,128)(2,1)S(1)}, u32[]{:S(2)}, u32[]{:S(2)}) %collective-permute-start.4) | collective-permute-done | bytes 98336 | tf_op jit(solution)/shard_map/ppermute | solution.py:222
  14.9 0.9 broadcast_select_fusion.1
  15.9 0.7 pad_maximum_fusion.1
  16.6 0.0 all-gather.2.cloned.1.call-update
  16.6 2.2 %shard_map.113 = (bf16[1544,128]{1,0:T(8,128)(2,1)}, bf16[1544,128]{1,0:T(8,128)(2,1)}) custom-call(s32[1,1]{1,0:T(1,128)} %bitcast.core_ref, bf16[1,128,2048]{2,1,0:T(8,128)(2,1)} %q_ref.1, bf16[1,128,512]{2,1,0:T(8,128)(2,1)} %k_ref.1, bf16[1,128,512]{2,1,0:T(8,128)(2,1)} %v_ref.1, s32[1,128]{1,0:T(1,128)} %doc_ref.1), custom_call_target="tpu_custom_call" | custom-call | bytes 1577476 | tf_op jit(solution)/shard_map/pallas_call | solution.py:38
  18.8 9.3 %collective-permute-start = (bf16[1544,128]{1,0:T(8,128)(2,1)}, bf16[1544,128]{1,0:T(8,128)(2,1)S(1)}, u32[]{:S(2)}, u32[]{:S(2)}) collective-permute-start(bf16[1544,128]{1,0:T(8,128)(2,1)} %get-tuple-element.15), channel_id=1, source_target_pairs={{0,32},{32,0},{1,33},{33,1},{2,34},{34,2},{3,35},{35,3},{4,36},{36... | collective-permute-start | bytes 1185800 | tf_op jit(solution)/shard_map/ppermute | solution.py:222
  28.1 0.9 slice.6
  29.0 0.6 collective-permute-done.other_ref
  29.6 0.0 copy-start.6
  29.7 1.6 %broadcast_in_dim.2 = bf16[8,1040,128]{2,1,0:T(8,128)(2,1)} broadcast(bf16[1040,128]{1,0:T(8,128)(2,1)S(1)} %pad_maximum_fusion), dimensions={1,2} | broadcast | bytes 2396160 | tf_op jit(solution)/shard_map/broadcast_in_dim | solution.py:252
  31.3 0.0 copy-start.7
  31.3 0.0 copy-start.8
  31.3 0.0 copy-done.6
  31.3 3.7 %all-to-all-start = ((bf16[8,1040,128]{2,1,0:T(8,128)(2,1)}), bf16[8,1040,128]{2,1,0:T(8,128)(2,1)S(1)}, u32[]{:S(2)}, u32[]{:S(2)}) async-start(bf16[8,1040,128]{2,1,0:T(8,128)(2,1)} %broadcast_in_dim.2), calls=%async_computation | async-start | bytes 4259840 | tf_op jit(solution)/shard_map/all_to_all | solution.py:218
  35.1 0.0 copy-done.7
  35.1 0.7 copy.12.route_ref
  35.8 0.0 copy-done.8
  35.8 0.7 copy.13.rw_ref
  36.5 2.5 %shard_map.114 = bf16[128,2176]{1,0:T(8,128)(2,1)} custom-call(s32[1,128,2]{2,1,0:T(8,128)} %copy.12.route_ref, bf16[1,128,2]{2,1,0:T(8,128)(2,1)} %copy.13.rw_ref, bf16[1,128,2048]{2,1,0:T(8,128)(2,1)} %cot_ref.1), custom_call_target="tpu_custom_call" | custom-call | bytes 1082880 | tf_op jit(solution)/shard_map/pallas_call | solution.py:38
  39.0 0.7 add_bitcast_fusion.base_ref
  39.7 23.9 %all-to-all-done = bf16[8,1040,128]{2,1,0:T(8,128)(2,1)S(1)} async-done(((bf16[8,1040,128]{2,1,0:T(8,128)(2,1)}), bf16[8,1040,128]{2,1,0:T(8,128)(2,1)S(1)}, u32[]{:S(2)}, u32[]{:S(2)}) %all-to-all-start) | async-done | bytes 2129952 | tf_op jit(solution)/shard_map/all_to_all | solution.py:218
  63.5 0.0 copy-start.1
  63.5 3.6 %all-to-all-start.2 = ((bf16[16,8,2176]{2,1,0:T(8,128)(2,1)}), bf16[16,8,2176]{2,1,0:T(8,128)(2,1)S(1)}, u32[]{:S(2)}, u32[]{:S(2)}) async-start(bf16[16,8,2176]{2,1,0:T(8,128)(2,1)} %bitcast.16), calls=%async_computation.2 | async-start | bytes 1114112 | tf_op jit(solution)/shard_map/all_to_all | solution.py:218
  67.1 0.0 copy-done.1
  67.1 8.5 %shard_map.115 = (bf16[128,1024]{1,0:T(8,128)(2,1)}, bf16[128,1024]{1,0:T(8,128)(2,1)}) custom-call(s32[1,2]{1,0:T(1,128)} %add_bitcast_fusion.base_ref, bf16[1544,128]{1,0:T(8,128)(2,1)} %get-tuple-element.14.own_ref, bf16[1544,128]{1,0:T(8,128)(2,1)} %copy-done.6, bf16[16,520,128]{2,1,0:T(8,128)(2,1)} %bitcast.19), custom_call_target="tpu_custom_call" | custom-call | flops 4294967296 | bytes 3444744 | tf_op jit(solution)/shard_map/pallas_call | solution.py:38
  75.6 3.2 %collective-permute-start.1 = (bf16[128,1024]{1,0:T(8,128)(2,1)}, bf16[128,1024]{1,0:T(8,128)(2,1)S(1)}, u32[]{:S(2)}, u32[]{:S(2)}) collective-permute-start(bf16[128,1024]{1,0:T(8,128)(2,1)} %get-tuple-element.18), channel_id=1, source_target_pairs={{0,32},{32,0},{1,33},{33,1},{2,34},{34,2},{3,35},{35,3},{4,36},{36... | collective-permute-start | bytes 786440 | tf_op jit(solution)/shard_map/ppermute | solution.py:222
  78.8 1.4 collective-permute-done.1.other_ref
  80.1 0.0 copy-start.5
  80.2 0.7 copy-done.5
  80.9 2.4 %shard_map.116 = (bf16[1,128,2048]{2,1,0:T(8,128)(2,1)}, bf16[128,2048]{1,0:T(8,128)(2,1)}) custom-call(s32[1,1]{1,0:T(1,128)} %bitcast.core_ref, bf16[128,1024]{1,0:T(8,128)(2,1)} %get-tuple-element.17.own_ref, bf16[128,1024]{1,0:T(8,128)(2,1)} %copy-done.5, s32[1,128,2]{2,1,0:T(8,128)} %copy.12.route_ref), custom_call_target="tpu_custom_call" | custom-call | bytes 1573892 | tf_op jit(solution)/shard_map/pallas_call | solution.py:38
  83.2 0.0 all-to-all-done.2
  83.2 0.0 copy-start
  83.2 6.9 %all-to-all-start.1 = ((bf16[16,8,2048]{2,1,0:T(8,128)(2,1)}), bf16[16,8,2048]{2,1,0:T(8,128)(2,1)S(1)}, u32[]{:S(2)}, u32[]{:S(2)}) async-start(bf16[16,8,2048]{2,1,0:T(8,128)(2,1)} %bitcast.22), calls=%async_computation.1 | async-start | bytes 1048576 | tf_op jit(solution)/shard_map/all_to_all | solution.py:218
  90.1 2.6 %collective-permute-start.3 = (bf16[128,2176]{1,0:T(8,128)(2,1)S(1)}, bf16[128,2176]{1,0:T(8,128)(2,1)S(1)}, u32[]{:S(2)}, u32[]{:S(2)}) collective-permute-start(bf16[128,2176]{1,0:T(8,128)(2,1)S(1)} %bitcast.17), channel_id=1, source_target_pairs={{0,32},{32,0},{1,33},{33,1},{2,34},{34,2},{3,35},{35,3},{4,36},{36... | collective-permute-start | bytes 1671176 | tf_op jit(solution)/shard_map/ppermute | solution.py:222
  92.7 8.2 %all-to-all-done.1 = bf16[16,8,2048]{2,1,0:T(8,128)(2,1)S(1)} async-done(((bf16[16,8,2048]{2,1,0:T(8,128)(2,1)}), bf16[16,8,2048]{2,1,0:T(8,128)(2,1)S(1)}, u32[]{:S(2)}, u32[]{:S(2)}) %all-to-all-start.1) | async-done | bytes 524320 | tf_op jit(solution)/shard_map/all_to_all | solution.py:218
  100.8 0.0 copy-start.2
  100.8 3.6 %collective-permute-start.2 = (bf16[128,2048]{1,0:T(8,128)(2,1)S(1)}, bf16[128,2048]{1,0:T(8,128)(2,1)S(1)}, u32[]{:S(2)}, u32[]{:S(2)}) collective-permute-start(bf16[128,2048]{1,0:T(8,128)(2,1)S(1)} %bitcast.20), channel_id=1, source_target_pairs={{0,32},{32,0},{1,33},{33,1},{2,34},{34,2},{3,35},{35,3},{4,36},{36... | collective-permute-start | bytes 1572872 | tf_op jit(solution)/shard_map/ppermute | solution.py:222
  104.5 0.0 collective-permute-done.3.dy2_ref
  104.5 0.0 copy-start.3
  104.5 1.5 %collective-permute-done.2.x2_ref = bf16[128,2048]{1,0:T(8,128)(2,1)S(1)} collective-permute-done((bf16[128,2048]{1,0:T(8,128)(2,1)S(1)}, bf16[128,2048]{1,0:T(8,128)(2,1)S(1)}, u32[]{:S(2)}, u32[]{:S(2)}) %collective-permute-start.2) | collective-permute-done | bytes 524320 | tf_op jit(solution)/shard_map/ppermute | solution.py:222
  106.0 0.0 copy-start.4
  106.0 0.0 all-gather.2.cloned.1.call-done
  106.0 0.0 copy-done
  106.0 0.0 copy-done.2
  106.0 0.0 copy-done.3
  106.0 0.8 copy-done.4
  106.8 6.4 %shard_map.118 = (f32[128,2048]{1,0:T(8,128)}, bf16[128,2048]{1,0:T(8,128)(2,1)}) custom-call(bf16[128,2048]{1,0:T(8,128)(2,1)} %bitcast.21, bf16[128,2048]{1,0:T(8,128)(2,1)} %copy-done.4, bf16[128,2176]{1,0:T(8,128)(2,1)} %bitcast.18, bf16[128,2176]{1,0:T(8,128)(2,1)} %copy-done.3, bf16[32,192,256]{2,1,0:T(8,128)(2,1)} %bitcast.15), custom_call_target="tpu_custom_call" | custom-call | flops 1342177280 | bytes 6881280 | tf_op jit(solution)/shard_map/pallas_call | solution.py:38
  113.2 2.3 %collective-permute-start.5 = (bf16[128,2048]{1,0:T(8,128)(2,1)}, bf16[128,2048]{1,0:T(8,128)(2,1)S(1)}, u32[]{:S(2)}, u32[]{:S(2)}) collective-permute-start(bf16[128,2048]{1,0:T(8,128)(2,1)} %get-tuple-element.25), channel_id=1, source_target_pairs={{0,32},{32,0},{1,33},{33,1},{2,34},{34,2},{3,35},{35,3},{4,36},{36... | collective-permute-start | bytes 1572872 | tf_op jit(solution)/shard_map/ppermute | solution.py:222
  115.5 1.7 %collective-permute-done.5 = bf16[128,2048]{1,0:T(8,128)(2,1)S(1)} collective-permute-done((bf16[128,2048]{1,0:T(8,128)(2,1)}, bf16[128,2048]{1,0:T(8,128)(2,1)S(1)}, u32[]{:S(2)}, u32[]{:S(2)}) %collective-permute-start.5) | collective-permute-done | bytes 524320 | tf_op jit(solution)/shard_map/ppermute | solution.py:222
  117.2 1.3 fusion
  118.6 14.2 %all_to_all.37.part_ref = bf16[16,8,2048]{2,1,0:T(8,128)(2,1)} all-to-all(bf16[16,8,2048]{2,1,0:T(8,128)(2,1)S(1)} %fusion), channel_id=1, replica_groups=mesh['y'=4,'xh'=2,'core'=2,'z'=16,'xl'=2] {'y','xh','xl'}, dimensions={0} | all-to-all | bytes 1048576 | tf_op jit(solution)/shard_map/all_to_all | solution.py:218
  132.8 2.7 %shard_map.119 = bf16[1,128,2048]{2,1,0:T(8,128)(2,1)} custom-call(bf16[1,128,2048]{2,1,0:T(8,128)(2,1)} %get-tuple-element.12.attn_ref, s32[1,128,2]{2,1,0:T(8,128)} %copy.12.route_ref, bf16[16,8,2048]{2,1,0:T(8,128)(2,1)} %all_to_all.37.part_ref), custom_call_target="tpu_custom_call" | custom-call | bytes 1573888 | tf_op jit(solution)/shard_map/pallas_call | solution.py:38
  (2 shorter events, 0.0 us)
Async XLA Ops:
  7.2 98.8 %all-gather.2.cloned.1.call-start = ((), (), s32[]{:S(2)}) async-start(), calls=%async_computation.4 | async-start | bytes 3342336 | tf_op jit(solution)/shard_map/all_gather | solution.py:242
  8.8 6.1 %collective-permute-start.4 = (bf16[192,256]{1,0:T(8,128)(2,1)}, bf16[192,256]{1,0:T(8,128)(2,1)S(1)}, u32[]{:S(2)}, u32[]{:S(2)}) collective-permute-start(bf16[192,256]{1,0:T(8,128)(2,1)} %get-tuple-element.23), channel_id=1, source_target_pairs={{0,1},{1,0},{2,3},{3,2},{4,5},{5,4},{6,7},{7,6},{8,9},{9,8},{10,11... | collective-permute-start | bytes 294920 | tf_op jit(solution)/shard_map/ppermute | solution.py:222
  18.8 10.9 %collective-permute-start = (bf16[1544,128]{1,0:T(8,128)(2,1)}, bf16[1544,128]{1,0:T(8,128)(2,1)S(1)}, u32[]{:S(2)}, u32[]{:S(2)}) collective-permute-start(bf16[1544,128]{1,0:T(8,128)(2,1)} %get-tuple-element.15), channel_id=1, source_target_pairs={{0,32},{32,0},{1,33},{33,1},{2,34},{34,2},{3,35},{35,3},{4,36},{36... | collective-permute-start | bytes 1185800 | tf_op jit(solution)/shard_map/ppermute | solution.py:222
  29.6 1.7 %copy-start.6 = (bf16[1544,128]{1,0:T(8,128)(2,1)}, bf16[1544,128]{1,0:T(8,128)(2,1)S(1)}, u32[]{:S(2)}) copy-start(bf16[1544,128]{1,0:T(8,128)(2,1)S(1)} %collective-permute-done.other_ref) | copy-start | bytes 1185796
  31.3 3.8 %copy-start.7 = (s32[1,128,2]{1,2,0:T(2,128)S(1)}, s32[1,128,2]{1,2,0:T(2,128)}, u32[]{:S(2)}) copy-start(s32[1,128,2]{1,2,0:T(2,128)} %param.14) | copy-start | bytes 3076
  31.3 4.5 %copy-start.8 = (bf16[1,128,2]{1,2,0:T(2,128)(2,1)S(1)}, bf16[1,128,2]{1,2,0:T(2,128)(2,1)}, u32[]{:S(2)}) copy-start(bf16[1,128,2]{1,2,0:T(2,128)(2,1)} %param.15) | copy-start | bytes 1540
  31.3 32.2 %all-to-all-start = ((bf16[8,1040,128]{2,1,0:T(8,128)(2,1)}), bf16[8,1040,128]{2,1,0:T(8,128)(2,1)S(1)}, u32[]{:S(2)}, u32[]{:S(2)}) async-start(bf16[8,1040,128]{2,1,0:T(8,128)(2,1)} %broadcast_in_dim.2), calls=%async_computation | async-start | bytes 4259840 | tf_op jit(solution)/shard_map/all_to_all | solution.py:218
  63.5 3.6 %copy-start.1 = (bf16[8,1040,128]{2,1,0:T(8,128)(2,1)}, bf16[8,1040,128]{2,1,0:T(8,128)(2,1)S(1)}, u32[]{:S(2)}) copy-start(bf16[8,1040,128]{2,1,0:T(8,128)(2,1)S(1)} %all-to-all-done) | copy-start | bytes 6389764
  63.5 19.7 %all-to-all-start.2 = ((bf16[16,8,2176]{2,1,0:T(8,128)(2,1)}), bf16[16,8,2176]{2,1,0:T(8,128)(2,1)S(1)}, u32[]{:S(2)}, u32[]{:S(2)}) async-start(bf16[16,8,2176]{2,1,0:T(8,128)(2,1)} %bitcast.16), calls=%async_computation.2 | async-start | bytes 1114112 | tf_op jit(solution)/shard_map/all_to_all | solution.py:218
  75.6 4.6 %collective-permute-start.1 = (bf16[128,1024]{1,0:T(8,128)(2,1)}, bf16[128,1024]{1,0:T(8,128)(2,1)S(1)}, u32[]{:S(2)}, u32[]{:S(2)}) collective-permute-start(bf16[128,1024]{1,0:T(8,128)(2,1)} %get-tuple-element.18), channel_id=1, source_target_pairs={{0,32},{32,0},{1,33},{33,1},{2,34},{34,2},{3,35},{35,3},{4,36},{36... | collective-permute-start | bytes 786440 | tf_op jit(solution)/shard_map/ppermute | solution.py:222
  80.1 0.7 copy-start.5
  83.2 22.8 %copy-start = (bf16[16,8,2176]{2,1,0:T(8,128)(2,1)}, bf16[16,8,2176]{2,1,0:T(8,128)(2,1)S(1)}, u32[]{:S(2)}) copy-start(bf16[16,8,2176]{2,1,0:T(8,128)(2,1)S(1)} %all-to-all-done.2) | copy-start | bytes 1671172
  83.2 17.6 %all-to-all-start.1 = ((bf16[16,8,2048]{2,1,0:T(8,128)(2,1)}), bf16[16,8,2048]{2,1,0:T(8,128)(2,1)S(1)}, u32[]{:S(2)}, u32[]{:S(2)}) async-start(bf16[16,8,2048]{2,1,0:T(8,128)(2,1)} %bitcast.22), calls=%async_computation.1 | async-start | bytes 1048576 | tf_op jit(solution)/shard_map/all_to_all | solution.py:218
  90.1 14.4 %collective-permute-start.3 = (bf16[128,2176]{1,0:T(8,128)(2,1)S(1)}, bf16[128,2176]{1,0:T(8,128)(2,1)S(1)}, u32[]{:S(2)}, u32[]{:S(2)}) collective-permute-start(bf16[128,2176]{1,0:T(8,128)(2,1)S(1)} %bitcast.17), channel_id=1, source_target_pairs={{0,32},{32,0},{1,33},{33,1},{2,34},{34,2},{3,35},{35,3},{4,36},{36... | collective-permute-start | bytes 1671176 | tf_op jit(solution)/shard_map/ppermute | solution.py:222
  100.8 5.2 %copy-start.2 = (bf16[16,8,2048]{2,1,0:T(8,128)(2,1)}, bf16[16,8,2048]{2,1,0:T(8,128)(2,1)S(1)}, u32[]{:S(2)}) copy-start(bf16[16,8,2048]{2,1,0:T(8,128)(2,1)S(1)} %all-to-all-done.1) | copy-start | bytes 1572868
  100.8 5.2 %collective-permute-start.2 = (bf16[128,2048]{1,0:T(8,128)(2,1)S(1)}, bf16[128,2048]{1,0:T(8,128)(2,1)S(1)}, u32[]{:S(2)}, u32[]{:S(2)}) collective-permute-start(bf16[128,2048]{1,0:T(8,128)(2,1)S(1)} %bitcast.20), channel_id=1, source_target_pairs={{0,32},{32,0},{1,33},{33,1},{2,34},{34,2},{3,35},{35,3},{4,36},{36... | collective-permute-start | bytes 1572872 | tf_op jit(solution)/shard_map/ppermute | solution.py:222
  104.5 1.5 %copy-start.3 = (bf16[128,2176]{1,0:T(8,128)(2,1)}, bf16[128,2176]{1,0:T(8,128)(2,1)S(1)}, u32[]{:S(2)}) copy-start(bf16[128,2176]{1,0:T(8,128)(2,1)S(1)} %collective-permute-done.3.dy2_ref) | copy-start | bytes 1671172
  106.0 0.8 copy-start.4
  113.2 4.0 %collective-permute-start.5 = (bf16[128,2048]{1,0:T(8,128)(2,1)}, bf16[128,2048]{1,0:T(8,128)(2,1)S(1)}, u32[]{:S(2)}, u32[]{:S(2)}) collective-permute-start(bf16[128,2048]{1,0:T(8,128)(2,1)} %get-tuple-element.25), channel_id=1, source_target_pairs={{0,32},{32,0},{1,33},{33,1},{2,34},{34,2},{3,35},{35,3},{4,36},{36... | collective-permute-start | bytes 1572872 | tf_op jit(solution)/shard_map/ppermute | solution.py:222
Sparse Core Ops, SparseCore 0:
  16.7 72.4 all-gather.1

commit v3 on v2

--- a/solution.py
+++ b/solution.py
@@ -66,8 +66,17 @@
         write(send_ref, keep_ref)
 
 
-def pack_heads(core_ref, q_ref, k_ref, v_ref, doc_ref, keep_ref, send_ref):
-    docs = jnp.broadcast_to(doc_ref[...].astype(F32), (8, TOK)).astype(BF16)
+def pack_heads(core_ref, q_ref, k_ref, v_ref, doc_ref, route_ref, keep_ref, send_ref):
+    docs = jnp.broadcast_to(doc_ref[...].astype(F32), (4, TOK))
+    hits = jnp.where(route_ref[0] == 0, 1.0, 0.0)
+    routed = jnp.max(hits, axis=0, keepdims=True)
+    rows = lax.broadcasted_iota(jnp.int32, (TOK, TOK), 0)
+    cols = lax.broadcasted_iota(jnp.int32, (TOK, TOK), 1)
+    upto = jnp.where(rows <= cols, 1.0, 0.0).astype(BF16)
+    wide = jnp.broadcast_to(routed, (8, TOK)).astype(BF16)
+    count = jnp.dot(wide, upto, preferred_element_type=F32)
+    slots = jnp.where(routed > 0.5, count - 1.0, -1.0)
+    docs = jnp.concatenate([docs, slots[:4]], axis=0).astype(BF16)
     core = core_ref[0, 0]
     for side, out_ref in ((core, keep_ref), (1 - core, send_ref)):
         row = 0
@@ -79,7 +88,13 @@
         out_ref[row:, :] = docs
 
 
-def attend(base_ref, own_ref, other_ref, kv_ref, keep_ref, send_ref, k_aug, v_aug):
+def spread(keep_ref, got_ref, out_ref):
+    for i in range(out_ref.shape[0]):
+        out_ref[i, 0] = keep_ref[QW:, :]
+        out_ref[i, 1] = got_ref[QW:, :]
+
+
+def attend(base_ref, own_ref, other_ref, kv_ref, keep_ref, send_ref, pay_ref, k_aug, v_aug):
     length = k_aug.shape[1]
     heads = KW // HEAD_DIM
     docs = kv_ref[:, 2 * heads * TOK :, :].astype(F32)
@@ -106,10 +121,17 @@
     mine = (mine + base_ref[0, 0]).astype(F32)
     q_doc = jnp.where((mine >= first) & (mine < after), 1.0, 0.0).astype(BF16)
     factor = HEAD_DIM**-0.5 * LOG2E
+    place = lax.broadcasted_iota(jnp.int32, (CAP, TOK), 0).astype(F32)
+    picks = []
+    for ref in (own_ref, other_ref):
+        slots = ref[QW + 2 * KW :, :].astype(F32)[4:5]
+        picks.append(jnp.where(place == slots, 1.0, 0.0).astype(BF16))
+    chosen = [[], []]
     for h in range(HEADS // 2):
         g = h // (HEADS // KV_HEADS)
         here = slice(h * HEAD_DIM, (h + 1) * HEAD_DIM)
-        q = jnp.concatenate([own_ref[h * TOK : (h + 1) * TOK], other_ref[h * TOK : (h + 1) * TOK]], axis=0)
+        rows = slice(h * TOK, (h + 1) * TOK)
+        q = jnp.concatenate([own_ref[rows], other_ref[rows]], axis=0)
         q = jnp.concatenate([q, q_doc], axis=1)
         scores = lax.dot_general(q, k_aug[g], NT, preferred_element_type=F32)
         top = jnp.max(scores, axis=1, keepdims=True)
@@ -118,6 +140,10 @@
         mixed = (mixed[:, :HEAD_DIM] / mixed[:, HEAD_DIM:]).astype(BF16)
         keep_ref[:, here] = mixed[:TOK]
         send_ref[:, here] = mixed[TOK:]
+        for i, part in enumerate((mixed[:TOK], mixed[TOK:])):
+            got = jnp.dot(picks[i], part, preferred_element_type=F32)
+            chosen[i].append(got.astype(BF16))
+    copies(jnp.concatenate(chosen[0] + chosen[1], axis=1), pay_ref)
 
 
 def selection(route_ref, width):
@@ -158,44 +184,65 @@
     copies(jnp.concatenate([take(select, cot_ref[0]), take(select, weight)], axis=1), pay_ref)
 
 
-def send_slots(core_ref, own_ref, other_ref, route_ref, attn_ref, pay_ref):
+def join(core_ref, own_ref, other_ref, attn_ref):
     core = core_ref[0, 0]
     for side, ref in ((core, own_ref), (1 - core, other_ref)):
         attn_ref[0, :, pl.ds(pl.multiple_of(side * QW, QW), QW)] = ref[...]
-    _, scaled = normalized(attn_ref[0].astype(F32))
-    select, _ = selection(route_ref, 1)
-    copies(take(select, scaled.astype(BF16)), pay_ref)
-
-
-def expert(x_ref, x2_ref, dy_ref, dy2_ref, w_ref, own_out, other_out, panels, sems):
-    depth = panels.shape[2]
-    loads = [
-        pltpu.make_async_copy(w_ref.at[:, pl.ds(i * depth, depth), :], panels.at[i], sems.at[i])
-        for i in range(3)
-    ]
+
+
+def expert(ids_ref, x_ref, x2_ref, dy_ref, dy2_ref, w_ref, own_out, other_out, panels, sems):
+    core, side = ids_ref[0, 0], ids_ref[0, 1]
+    depth = panels.shape[3]
+    loads = {}
     for i in (2, 0, 1):
-        loads[i].start()
-
-    def panel(i):
-        return panels[i].reshape(D, HALF)
-
+        for s in range(2):
+            loads[i, s] = pltpu.make_async_copy(
+                w_ref.at[:, side ^ s, pl.ds(i * depth, depth), :],
+                panels.at[i, :, s],
+                sems.at[i, s],
+            )
+            loads[i, s].start()
+
+    def panel(i, half):
+        blocks = panels.shape[1] // 2
+        start = pl.multiple_of(half * blocks, blocks)
+        return panels[i, pl.ds(start, blocks)].reshape(QW, HALF)
+
+    def ready(i):
+        loads[i, 0].wait()
+        loads[i, 1].wait()
+
+    sides = (core, 1 - core)
+    attn = (
+        jnp.concatenate([x_ref[:, :QW], x_ref[:, QW:]], axis=0).astype(F32),
+        jnp.concatenate([x2_ref[:, QW:], x2_ref[:, :QW]], axis=0).astype(F32),
+    )
+    square = sum(jnp.sum(a * a, axis=1, keepdims=True) for a in attn) * (1.0 / D)
+    inverse = lax.rsqrt(square + EPS)
+    x = [(a * inverse).astype(BF16) for a in attn]
     dy = jnp.concatenate([dy_ref[...], dy2_ref[...]], axis=0)
-    x = jnp.concatenate([x_ref[...], x2_ref[...]], axis=0)
-    loads[2].wait()
-    back = jnp.dot(dy[:, :D], panel(2), preferred_element_type=F32)
+    ready(2)
+    back = jnp.dot(dy[:, :D], panels[2].reshape(D, HALF), preferred_element_type=F32)
     back = back * dy[:, D : D + 1].astype(F32)
-    loads[0].wait()
-    gate = jnp.dot(x, panel(0), preferred_element_type=F32)
-    loads[1].wait()
-    up = jnp.dot(x, panel(1), preferred_element_type=F32)
+
+    def forward(i):
+        ready(i)
+        first = jnp.dot(x[0], panel(i, sides[0]), preferred_element_type=F32)
+        return first + jnp.dot(x[1], panel(i, sides[1]), preferred_element_type=F32)
+
+    gate, up = forward(0), forward(1)
     sg = jax.nn.sigmoid(gate)
     grad_gate = (back * up * sg * (1.0 + gate * (1.0 - sg))).astype(BF16)
     grad_up = (back * gate * sg).astype(BF16)
-    part = lax.dot_general(grad_gate, panel(0), NT, preferred_element_type=F32)
-    part = part + lax.dot_general(grad_up, panel(1), NT, preferred_element_type=F32)
-    half = own_out.shape[0]
-    own_out[...] = part[:half]
-    other_out[...] = part[half:].astype(BF16)
+    rows = own_out.shape[0]
+    for half in range(2):
+        part = lax.dot_general(grad_gate, panel(0, half), NT, preferred_element_type=F32)
+        part = part + lax.dot_general(
+            grad_up, panel(1, half), NT, preferred_element_type=F32
+        )
+        here = slice(half * QW, (half + 1) * QW)
+        own_out[:, here] = part[:rows]
+        other_out[:, here] = part[rows:].astype(BF16)
 
 
 def finish(attn_ref, route_ref, part_ref, out_ref):
@@ -237,20 +284,26 @@
         pack_weights, (half, half), scalars(side), gate_w, up_w, down_w.T, smem=1
     )
     got_w = swap(send_w, "xl")
-    low = jnp.where(side == 0, keep_w, got_w)
-    high = jnp.where(side == 0, got_w, keep_w)
-    panels = lax.all_gather(jnp.concatenate([low, high]), "z", axis=0, tiled=True)
-    panels = panels.reshape(-1, 3 * rows, HALF)
-
     block = QW + 2 * KW + 8
     packed = shape((block, HEAD_DIM), BF16)
     keep, send = call(
-        pack_heads, (packed, packed), scalars(core), q, k, v, doc_ids, smem=1
-    )
+        pack_heads,
+        (packed, packed),
+        scalars(core),
+        q,
+        k,
+        v,
+        doc_ids,
+        jnp.swapaxes(routes, 1, 2),
+        smem=1,
+    )
+    keep, got_w = lax.optimization_barrier((keep, got_w))
+    panels = lax.all_gather(jnp.concatenate([keep_w, got_w]), "z", axis=0, tiled=True)
+    panels = panels.reshape(-1, 2, 3 * rows, HALF)
+
     got = swap(send, "core")
-    kv = jnp.concatenate([keep[QW:], got[QW:]])
-    kv = jnp.broadcast_to(kv[None], (chips, *kv.shape)).reshape(-1, HEAD_DIM)
-    kv = all_to_all(kv, CHIPS).reshape(-1, block - QW, HEAD_DIM)
+    kv = call(spread, shape((chips, 2, block - QW, HEAD_DIM), BF16), keep, got)
+    kv = all_to_all(kv.reshape(-1, HEAD_DIM), CHIPS).reshape(-1, block - QW, HEAD_DIM)
     length = kv.shape[0] * TOK
 
     dy = call(
@@ -261,9 +314,9 @@
     other_dy = swap(own_dy, "core")
 
     mixed = shape((TOK, QW), BF16)
-    keep_o, send_o = call(
+    keep_o, send_o, pay = call(
         attend,
-        (mixed, mixed),
+        (mixed, mixed, shape((peers * CAP, D), BF16)),
         scalars(lax.axis_index(CHIPS) * (2 * TOK), core * TOK),
         keep,
         got,
@@ -272,30 +325,26 @@
         flops=16 * TOK * length * QW,
         scratch_shapes=[pltpu.VMEM((2, length, 2 * HEAD_DIM), BF16)] * 2,
     )
-    attn, pay = call(
-        send_slots,
-        (shape((1, TOK, D), BF16), shape((peers * CAP, D), BF16)),
-        scalars(core),
-        keep_o,
-        swap(send_o, "core"),
-        routes,
-        smem=1,
-    )
     own_x = all_to_all(pay, PEERS)
+    attn = call(
+        join, shape((1, TOK, D), BF16), scalars(core), keep_o, swap(send_o, "core"), smem=1
+    )
     other_x = swap(own_x, "core")
     own_part, other_part = call(
         expert,
         (shape((peers * CAP, D), F32), shape((peers * CAP, D), BF16)),
+        scalars(core, side),
         own_x,
         other_x,
         own_dy,
         other_dy,
         panels,
+        smem=1,
         hbm=1,
         flops=20 * peers * CAP * D * HALF,
         scratch_shapes=[
-            pltpu.VMEM((3, panels.shape[0], rows, HALF), BF16),
-            pltpu.SemaphoreType.DMA((3,)),
+            pltpu.VMEM((3, panels.shape[0], 2, rows, HALF), BF16),
+            pltpu.SemaphoreType.DMA((3, 2)),
         ],
     )
     part = (own_part + swap(other_part, "core").astype(F32)).astype(BF16)

time: 143 us -> 144 us (level)
  blocking collectives: 14.2 us -> 0 us
  Pallas kernels: 26.2 us -> 34.2 us
  starting transfers between devices: 39.1 us -> 43.8 us
  waiting for transfers between devices: 39.4 us -> 40.9 us
    all_to_all x1 -> x0, blocking collectives: 14.2 us -> none  [all_to_all(): return lax.all_to_all(x, axes, 0, 0, tiled=True)]
    pallas_call x7 -> x8, Pallas kernels: 26.2 us -> 34.2 us  [call(): pl.pallas_call(kernel, out_shape=out_shape, in_specs=specs, out_specs=jax...]
    all_to_all x3 -> x4, waiting for transfers between devices: 32 us -> 35.7 us  [all_to_all(): return lax.all_to_all(x, axes, 0, 0, tiled=True)]
    all_to_all x3 -> x4, starting transfers between devices: 14.2 us -> 17.5 us  [all_to_all(): return lax.all_to_all(x, axes, 0, 0, tiled=True)]
    ppermute x6, waiting for transfers between devices: 7.39 us -> 5.17 us  [swap(): return lax.ppermute(x, axis, [(0, 1), (1, 0)])]
    unnamed x20 -> x24, local copies, waits for them, and re-layouts: 2.96 us -> 4.72 us
    broadcast_in_dim x1 -> x0, local copies, waits for them, and re-layouts: 1.63 us -> none  [on_device(): kv = jnp.broadcast_to(kv[None], (chips, *kv.shape)).reshape(-1, HEAD_DIM)]
  transfers between devices with their start and end apart: 10 -> 11, of which waited for: 7 -> 7; matrix products, arithmetic and copies ran while one was open for 3% -> 2% of each run, Pallas kernels for 11% -> 16%
where the time goes in v3:
time: 144 us; the launch traced here: 143 us
  starting transfers between devices  43.8 us (30%)
  waiting for transfers between devices  40.9 us (28%)
  Pallas kernels  34.2 us (24%)
  between operations  14.2 us (10%)
  other arithmetic  4.85 us (3%)
  local copies, waits for them, and re-layouts  4.72 us (3%)
    all_to_all x4, waiting for transfers between devices, all_to_all(): return lax.all_to_all(x, axes, 0, 0, tiled=True)  35.7 us
    pallas_call x8, Pallas kernels, call(): pl.pallas_call(kernel, out_shape=out_shape, in_specs=specs, out_specs=jax...  34.2 us
    ppermute x6, starting transfers between devices, swap(): return lax.ppermute(x, axis, [(0, 1), (1, 0)])  26.3 us
    all_to_all x4, starting transfers between devices, all_to_all(): return lax.all_to_all(x, axes, 0, 0, tiled=True)  17.5 us
    ppermute x6, waiting for transfers between devices, swap(): return lax.ppermute(x, axis, [(0, 1), (1, 0)])  5.17 us
    unnamed x24, local copies, waits for them, and re-layouts  4.72 us
  transfers between devices with their start and end apart: 11, of which 7 were waited for; matrix products, arithmetic and copies ran while one was open for 2% of the time, Pallas kernels for 16%

profile of v3, /device:TPU:1, one launch (start us, length us, event | category | flops | bytes accessed | tf_op | source)
XLA Modules:
  0.0 142.7 jit_solution(9796739520706461511)
XLA Ops:
  7.2 0.0 all-gather.2.cloned.1.call-start
  7.2 1.6 %shard_map.114 = (bf16[192,256]{1,0:T(8,128)(2,1)}, bf16[192,256]{1,0:T(8,128)(2,1)}) custom-call(s32[1,1]{1,0:T(1,128)} %bitcast.5.side_ref, bf16[64,448]{1,0:T(8,128)(2,1)} %gate_ref.1, bf16[64,448]{1,0:T(8,128)(2,1)} %up_ref.1, bf16[64,448]{1,0:T(8,128)(2,1)} %bitcast.30), custom_call_target="tpu_custom_call" | custom-call | bytes 368644 | tf_op jit(solution)/shard_map/pallas_call | solution.py:38
  8.8 3.9 %collective-permute-start = (bf16[192,256]{1,0:T(8,128)(2,1)}, bf16[192,256]{1,0:T(8,128)(2,1)S(1)}, u32[]{:S(2)}, u32[]{:S(2)}) collective-permute-start(bf16[192,256]{1,0:T(8,128)(2,1)} %get-tuple-element.16), channel_id=1, source_target_pairs={{0,1},{1,0},{2,3},{3,2},{4,5},{5,4},{6,7},{7,6},{8,9},{9,8},{10,11... | collective-permute-start | bytes 294920 | tf_op jit(solution)/shard_map/ppermute | solution.py:269
  12.7 2.2 %shard_map.113 = (bf16[1544,128]{1,0:T(8,128)(2,1)}, bf16[1544,128]{1,0:T(8,128)(2,1)}) custom-call(s32[1,1]{1,0:T(1,128)} %bitcast.core_ref, bf16[1,128,2048]{2,1,0:T(8,128)(2,1)} %q_ref.1, bf16[1,128,512]{2,1,0:T(8,128)(2,1)} %k_ref.1, bf16[1,128,512]{2,1,0:T(8,128)(2,1)} %v_ref.1, s32[1,128]{1,0:T(1,128)} %doc_ref.1, s32[1,2,128]{2,1,0:T(2,128)} %bitcast.31), custom_call_target="tpu_custom_call" | custom-call | bytes 1578500 | tf_op jit(solution)/shard_map/pallas_call | solution.py:38
  14.9 0.0 collective-permute-done
  14.9 1.6 %pad_maximum_fusion = bf16[384,256]{1,0:T(8,128)(2,1)} fusion(bf16[192,256]{1,0:T(8,128)(2,1)S(1)} %collective-permute-done, bf16[192,256]{1,0:T(8,128)(2,1)} %get-tuple-element.24), kind=kLoop, calls=%fused_computation.2 | loop fusion | flops 393216 | bytes 393216 | tf_op jit(solution)/shard_map/concatenate | solution.py:301
  16.5 0.0 all-gather.2.cloned.1.call-update
  16.6 9.3 %collective-permute-start.1 = (bf16[1544,128]{1,0:T(8,128)(2,1)}, bf16[1544,128]{1,0:T(8,128)(2,1)S(1)}, u32[]{:S(2)}, u32[]{:S(2)}) collective-permute-start(bf16[1544,128]{1,0:T(8,128)(2,1)} %get-tuple-element.18), channel_id=1, source_target_pairs={{0,32},{32,0},{1,33},{33,1},{2,34},{34,2},{3,35},{35,3},{4,36},{36... | collective-permute-start | bytes 1185800 | tf_op jit(solution)/shard_map/ppermute | solution.py:269
  25.9 1.5 %collective-permute-done.1.got_ref.other_ref = bf16[1544,128]{1,0:T(8,128)(2,1)S(1)} collective-permute-done((bf16[1544,128]{1,0:T(8,128)(2,1)}, bf16[1544,128]{1,0:T(8,128)(2,1)S(1)}, u32[]{:S(2)}, u32[]{:S(2)}) %collective-permute-start.1) | collective-permute-done | bytes 395296 | tf_op jit(solution)/shard_map/ppermute | solution.py:269
  27.4 0.0 copy-start.6
  27.4 0.8 copy-done.6
  28.2 2.8 %shard_map.116 = bf16[8,2,520,128]{3,2,1,0:T(8,128)(2,1)} custom-call(bf16[1544,128]{1,0:T(8,128)(2,1)} %get-tuple-element.17.keep_ref.own_ref, bf16[1544,128]{1,0:T(8,128)(2,1)} %copy-done.6), custom_call_target="tpu_custom_call" | custom-call | bytes 2920448 | tf_op jit(solution)/shard_map/pallas_call | solution.py:38
  30.9 0.0 copy-start.8
  30.9 0.0 copy-start.9
  30.9 3.7 %all-to-all-start = ((bf16[8,1040,128]{2,1,0:T(8,128)(2,1)}), bf16[8,1040,128]{2,1,0:T(8,128)(2,1)S(1)}, u32[]{:S(2)}, u32[]{:S(2)}) async-start(bf16[8,1040,128]{2,1,0:T(8,128)(2,1)} %bitcast.21), calls=%async_computation | async-start | bytes 4259840 | tf_op jit(solution)/shard_map/all_to_all | solution.py:265
  34.7 0.0 copy-done.8
  34.7 0.7 copy.12.route_ref
  35.4 0.0 copy-done.9
  35.4 0.7 copy.13.rw_ref
  36.2 2.4 %shard_map.115 = bf16[128,2176]{1,0:T(8,128)(2,1)} custom-call(s32[1,128,2]{2,1,0:T(8,128)} %copy.12.route_ref, bf16[1,128,2]{2,1,0:T(8,128)(2,1)} %copy.13.rw_ref, bf16[1,128,2048]{2,1,0:T(8,128)(2,1)} %cot_ref.1), custom_call_target="tpu_custom_call" | custom-call | bytes 1082880 | tf_op jit(solution)/shard_map/pallas_call | solution.py:38
  38.6 24.5 %all-to-all-done = bf16[8,1040,128]{2,1,0:T(8,128)(2,1)S(1)} async-done(((bf16[8,1040,128]{2,1,0:T(8,128)(2,1)}), bf16[8,1040,128]{2,1,0:T(8,128)(2,1)S(1)}, u32[]{:S(2)}, u32[]{:S(2)}) %all-to-all-start) | async-done | bytes 2129952 | tf_op jit(solution)/shard_map/all_to_all | solution.py:265
  63.1 0.0 copy-start.1
  63.1 3.6 %all-to-all-start.2 = ((bf16[16,8,2176]{2,1,0:T(8,128)(2,1)}), bf16[16,8,2176]{2,1,0:T(8,128)(2,1)S(1)}, u32[]{:S(2)}, u32[]{:S(2)}) async-start(bf16[16,8,2176]{2,1,0:T(8,128)(2,1)} %bitcast.23), calls=%async_computation.2 | async-start | bytes 1114112 | tf_op jit(solution)/shard_map/all_to_all | solution.py:265
  66.7 0.6 add_bitcast_fusion.base_ref
  67.3 0.0 copy-done.1
  67.3 14.0 %shard_map.117 = (bf16[128,1024]{1,0:T(8,128)(2,1)}, bf16[128,1024]{1,0:T(8,128)(2,1)}, bf16[128,2048]{1,0:T(8,128)(2,1)}) custom-call(s32[1,2]{1,0:T(1,128)} %add_bitcast_fusion.base_ref, bf16[1544,128]{1,0:T(8,128)(2,1)} %get-tuple-element.17.keep_ref.own_ref, bf16[1544,128]{1,0:T(8,128)(2,1)} %copy-done.6, bf16[16,520,128]{2,1,0:T(8,128)(2,1)} %bitcast.26), custom_call_target="tpu_custom_call" | custom-call | flops 4294967296 | bytes 3969032 | tf_op jit(solution)/shard_map/pallas_call | solution.py:38
  81.3 0.0 all-to-all-done.2
  81.4 0.0 copy-start
  81.4 6.6 %all-to-all-start.1 = ((bf16[16,8,2048]{2,1,0:T(8,128)(2,1)}), bf16[16,8,2048]{2,1,0:T(8,128)(2,1)S(1)}, u32[]{:S(2)}, u32[]{:S(2)}) async-start(bf16[16,8,2048]{2,1,0:T(8,128)(2,1)} %bitcast.29), calls=%async_computation.1 | async-start | bytes 1048576 | tf_op jit(solution)/shard_map/all_to_all | solution.py:265
  87.9 3.8 %collective-permute-start.4 = (bf16[128,2176]{1,0:T(8,128)(2,1)S(1)}, bf16[128,2176]{1,0:T(8,128)(2,1)S(1)}, u32[]{:S(2)}, u32[]{:S(2)}) collective-permute-start(bf16[128,2176]{1,0:T(8,128)(2,1)S(1)} %bitcast.24), channel_id=1, source_target_pairs={{0,32},{32,0},{1,33},{33,1},{2,34},{34,2},{3,35},{35,3},{4,36},{36... | collective-permute-start | bytes 1671176 | tf_op jit(solution)/shard_map/ppermute | solution.py:269
  91.7 6.2 %all-to-all-done.1 = bf16[16,8,2048]{2,1,0:T(8,128)(2,1)S(1)} async-done(((bf16[16,8,2048]{2,1,0:T(8,128)(2,1)}), bf16[16,8,2048]{2,1,0:T(8,128)(2,1)S(1)}, u32[]{:S(2)}, u32[]{:S(2)}) %all-to-all-start.1) | async-done | bytes 524320 | tf_op jit(solution)/shard_map/all_to_all | solution.py:265
  97.9 0.0 copy-start.3
  97.9 4.6 %collective-permute-start.3 = (bf16[128,2048]{1,0:T(8,128)(2,1)S(1)}, bf16[128,2048]{1,0:T(8,128)(2,1)S(1)}, u32[]{:S(2)}, u32[]{:S(2)}) collective-permute-start(bf16[128,2048]{1,0:T(8,128)(2,1)S(1)} %bitcast.27), channel_id=1, source_target_pairs={{0,32},{32,0},{1,33},{33,1},{2,34},{34,2},{3,35},{35,3},{4,36},{36... | collective-permute-start | bytes 1572872 | tf_op jit(solution)/shard_map/ppermute | solution.py:269
  102.6 0.6 add_bitcast_fusion.1.ids_ref
  103.1 0.8 collective-permute-done.3.x2_ref
  103.9 0.0 copy-start.5
  103.9 0.0 collective-permute-done.4.dy2_ref
  103.9 0.0 copy-start.4
  103.9 0.0 all-gather.2.cloned.1.call-done
  103.9 0.0 copy-done
  103.9 0.0 copy-done.3
  103.9 0.7 copy-done.5
  104.7 0.2 copy-done.4
  104.9 6.6 %shard_map.119 = (f32[128,2048]{1,0:T(8,128)}, bf16[128,2048]{1,0:T(8,128)(2,1)}) custom-call(s32[1,2]{1,0:T(1,128)} %add_bitcast_fusion.1.ids_ref, bf16[128,2048]{1,0:T(8,128)(2,1)} %bitcast.28, bf16[128,2048]{1,0:T(8,128)(2,1)} %copy-done.5, bf16[128,2176]{1,0:T(8,128)(2,1)} %bitcast.25, bf16[128,2176]{1,0:T(8,128)(2,1)} %copy-done.4, ...), custom_call_target="tpu_custom_call" | custom-call | flops 1342177280 | bytes 6881288 | tf_op jit(solution)/shard_map/pallas_call | solution.py:38
  111.5 0.0 copy-start.10
  111.5 2.4 %collective-permute-start.5 = (bf16[128,2048]{1,0:T(8,128)(2,1)}, bf16[128,2048]{1,0:T(8,128)(2,1)S(1)}, u32[]{:S(2)}, u32[]{:S(2)}) collective-permute-start(bf16[128,2048]{1,0:T(8,128)(2,1)} %get-tuple-element.27), channel_id=1, source_target_pairs={{0,32},{32,0},{1,33},{33,1},{2,34},{34,2},{3,35},{35,3},{4,36},{36... | collective-permute-start | bytes 1572872 | tf_op jit(solution)/shard_map/ppermute | solution.py:269
  113.9 1.7 %collective-permute-done.5 = bf16[128,2048]{1,0:T(8,128)(2,1)S(1)} collective-permute-done((bf16[128,2048]{1,0:T(8,128)(2,1)}, bf16[128,2048]{1,0:T(8,128)(2,1)S(1)}, u32[]{:S(2)}, u32[]{:S(2)}) %collective-permute-start.5) | collective-permute-done | bytes 524320 | tf_op jit(solution)/shard_map/ppermute | solution.py:269
  115.7 2.1 %fusion = bf16[16,8,2048]{2,1,0:T(8,128)(2,1)} fusion(f32[128,2048]{1,0:T(8,128)} %get-tuple-element.26, bf16[128,2048]{1,0:T(8,128)(2,1)S(1)} %collective-permute-done.5), kind=kLoop, calls=%fused_computation.1 | loop fusion | flops 786432 | bytes 2097152 | tf_op jit(solution)/shard_map/all_to_all | solution.py:265
  117.8 3.6 %all-to-all-start.3 = ((bf16[16,8,2048]{2,1,0:T(8,128)(2,1)}), bf16[16,8,2048]{2,1,0:T(8,128)(2,1)S(1)}, u32[]{:S(2)}, u32[]{:S(2)}) async-start(bf16[16,8,2048]{2,1,0:T(8,128)(2,1)} %fusion), calls=%async_computation.3 | async-start | bytes 1048576 | tf_op jit(solution)/shard_map/all_to_all | solution.py:265
  121.4 0.0 copy-done.10
  121.4 2.3 %collective-permute-start.2 = (bf16[128,1024]{1,0:T(8,128)(2,1)S(1)}, bf16[128,1024]{1,0:T(8,128)(2,1)S(1)}, u32[]{:S(2)}, u32[]{:S(2)}) collective-permute-start(bf16[128,1024]{1,0:T(8,128)(2,1)S(1)} %copy-done.10), channel_id=1, source_target_pairs={{0,32},{32,0},{1,33},{33,1},{2,34},{34,2},{3,35},{35,3},{4,36},{36... | collective-permute-start | bytes 786440 | tf_op jit(solution)/shard_map/ppermute | solution.py:269
  123.7 1.1 collective-permute-done.2.other_ref
  124.8 0.0 copy-start.7
  124.8 0.7 copy-done.7
  125.5 1.9 %shard_map.118.attn_ref = bf16[1,128,2048]{2,1,0:T(8,128)(2,1)} custom-call(s32[1,1]{1,0:T(1,128)} %bitcast.core_ref, bf16[128,1024]{1,0:T(8,128)(2,1)} %get-tuple-element.20.own_ref, bf16[128,1024]{1,0:T(8,128)(2,1)} %copy-done.7), custom_call_target="tpu_custom_call" | custom-call | bytes 1048580 | tf_op jit(solution)/shard_map/pallas_call | solution.py:38
  127.4 4.9 %all-to-all-done.3.part_ref = bf16[16,8,2048]{2,1,0:T(8,128)(2,1)S(1)} async-done(((bf16[16,8,2048]{2,1,0:T(8,128)(2,1)}), bf16[16,8,2048]{2,1,0:T(8,128)(2,1)S(1)}, u32[]{:S(2)}, u32[]{:S(2)}) %all-to-all-start.3) | async-done | bytes 524320 | tf_op jit(solution)/shard_map/all_to_all | solution.py:265
  132.3 0.0 copy-start.2
  132.3 0.8 copy-done.2
  133.1 2.7 %shard_map.120 = bf16[1,128,2048]{2,1,0:T(8,128)(2,1)} custom-call(bf16[1,128,2048]{2,1,0:T(8,128)(2,1)} %shard_map.118.attn_ref, s32[1,128,2]{2,1,0:T(8,128)} %copy.12.route_ref, bf16[16,8,2048]{2,1,0:T(8,128)(2,1)} %copy-done.2), custom_call_target="tpu_custom_call" | custom-call | bytes 1573888 | tf_op jit(solution)/shard_map/pallas_call | solution.py:38
Async XLA Ops:
  7.2 96.8 %all-gather.2.cloned.1.call-start = ((), (), s32[]{:S(2)}) async-start(), calls=%async_computation.4 | async-start | bytes 3342336 | tf_op jit(solution)/shard_map/all_gather | solution.py:301
  8.8 6.1 %collective-permute-start = (bf16[192,256]{1,0:T(8,128)(2,1)}, bf16[192,256]{1,0:T(8,128)(2,1)S(1)}, u32[]{:S(2)}, u32[]{:S(2)}) collective-permute-start(bf16[192,256]{1,0:T(8,128)(2,1)} %get-tuple-element.16), channel_id=1, source_target_pairs={{0,1},{1,0},{2,3},{3,2},{4,5},{5,4},{6,7},{7,6},{8,9},{9,8},{10,11... | collective-permute-start | bytes 294920 | tf_op jit(solution)/shard_map/ppermute | solution.py:269
  16.6 10.9 %collective-permute-start.1 = (bf16[1544,128]{1,0:T(8,128)(2,1)}, bf16[1544,128]{1,0:T(8,128)(2,1)S(1)}, u32[]{:S(2)}, u32[]{:S(2)}) collective-permute-start(bf16[1544,128]{1,0:T(8,128)(2,1)} %get-tuple-element.18), channel_id=1, source_target_pairs={{0,32},{32,0},{1,33},{33,1},{2,34},{34,2},{3,35},{35,3},{4,36},{36... | collective-permute-start | bytes 1185800 | tf_op jit(solution)/shard_map/ppermute | solution.py:269
  27.4 0.8 copy-start.6
  30.9 3.8 %copy-start.8 = (s32[1,128,2]{1,2,0:T(2,128)S(1)}, s32[1,128,2]{1,2,0:T(2,128)}, u32[]{:S(2)}) copy-start(s32[1,128,2]{1,2,0:T(2,128)} %param.14) | copy-start | bytes 3076
  30.9 4.5 %copy-start.9 = (bf16[1,128,2]{1,2,0:T(2,128)(2,1)S(1)}, bf16[1,128,2]{1,2,0:T(2,128)(2,1)}, u32[]{:S(2)}) copy-start(bf16[1,128,2]{1,2,0:T(2,128)(2,1)} %param.15) | copy-start | bytes 1540
  30.9 32.2 %all-to-all-start = ((bf16[8,1040,128]{2,1,0:T(8,128)(2,1)}), bf16[8,1040,128]{2,1,0:T(8,128)(2,1)S(1)}, u32[]{:S(2)}, u32[]{:S(2)}) async-start(bf16[8,1040,128]{2,1,0:T(8,128)(2,1)} %bitcast.21), calls=%async_computation | async-start | bytes 4259840 | tf_op jit(solution)/shard_map/all_to_all | solution.py:265
  63.1 4.2 %copy-start.1 = (bf16[8,1040,128]{2,1,0:T(8,128)(2,1)}, bf16[8,1040,128]{2,1,0:T(8,128)(2,1)S(1)}, u32[]{:S(2)}) copy-start(bf16[8,1040,128]{2,1,0:T(8,128)(2,1)S(1)} %all-to-all-done) | copy-start | bytes 6389764
  63.1 18.2 %all-to-all-start.2 = ((bf16[16,8,2176]{2,1,0:T(8,128)(2,1)}), bf16[16,8,2176]{2,1,0:T(8,128)(2,1)S(1)}, u32[]{:S(2)}, u32[]{:S(2)}) async-start(bf16[16,8,2176]{2,1,0:T(8,128)(2,1)} %bitcast.23), calls=%async_computation.2 | async-start | bytes 1114112 | tf_op jit(solution)/shard_map/all_to_all | solution.py:265
  81.4 22.6 %copy-start = (bf16[16,8,2176]{2,1,0:T(8,128)(2,1)}, bf16[16,8,2176]{2,1,0:T(8,128)(2,1)S(1)}, u32[]{:S(2)}) copy-start(bf16[16,8,2176]{2,1,0:T(8,128)(2,1)S(1)} %all-to-all-done.2) | copy-start | bytes 1671172
  81.4 16.6 %all-to-all-start.1 = ((bf16[16,8,2048]{2,1,0:T(8,128)(2,1)}), bf16[16,8,2048]{2,1,0:T(8,128)(2,1)S(1)}, u32[]{:S(2)}, u32[]{:S(2)}) async-start(bf16[16,8,2048]{2,1,0:T(8,128)(2,1)} %bitcast.29), calls=%async_computation.1 | async-start | bytes 1048576 | tf_op jit(solution)/shard_map/all_to_all | solution.py:265
  87.9 16.0 %collective-permute-start.4 = (bf16[128,2176]{1,0:T(8,128)(2,1)S(1)}, bf16[128,2176]{1,0:T(8,128)(2,1)S(1)}, u32[]{:S(2)}, u32[]{:S(2)}) collective-permute-start(bf16[128,2176]{1,0:T(8,128)(2,1)S(1)} %bitcast.24), channel_id=1, source_target_pairs={{0,32},{32,0},{1,33},{33,1},{2,34},{34,2},{3,35},{35,3},{4,36},{36... | collective-permute-start | bytes 1671176 | tf_op jit(solution)/shard_map/ppermute | solution.py:269
  97.9 6.0 %copy-start.3 = (bf16[16,8,2048]{2,1,0:T(8,128)(2,1)}, bf16[16,8,2048]{2,1,0:T(8,128)(2,1)S(1)}, u32[]{:S(2)}) copy-start(bf16[16,8,2048]{2,1,0:T(8,128)(2,1)S(1)} %all-to-all-done.1) | copy-start | bytes 1572868
  97.9 6.0 %collective-permute-start.3 = (bf16[128,2048]{1,0:T(8,128)(2,1)S(1)}, bf16[128,2048]{1,0:T(8,128)(2,1)S(1)}, u32[]{:S(2)}, u32[]{:S(2)}) collective-permute-start(bf16[128,2048]{1,0:T(8,128)(2,1)S(1)} %bitcast.27), channel_id=1, source_target_pairs={{0,32},{32,0},{1,33},{33,1},{2,34},{34,2},{3,35},{35,3},{4,36},{36... | collective-permute-start | bytes 1572872 | tf_op jit(solution)/shard_map/ppermute | solution.py:269
  103.9 0.8 copy-start.5
  103.9 1.0 copy-start.4
  111.5 9.9 %copy-start.10 = (bf16[128,1024]{1,0:T(8,128)(2,1)S(1)}, bf16[128,1024]{1,0:T(8,128)(2,1)}, u32[]{:S(2)}) copy-start(bf16[128,1024]{1,0:T(8,128)(2,1)} %get-tuple-element.21) | copy-start | bytes 786436
  111.5 4.1 %collective-permute-start.5 = (bf16[128,2048]{1,0:T(8,128)(2,1)}, bf16[128,2048]{1,0:T(8,128)(2,1)S(1)}, u32[]{:S(2)}, u32[]{:S(2)}) collective-permute-start(bf16[128,2048]{1,0:T(8,128)(2,1)} %get-tuple-element.27), channel_id=1, source_target_pairs={{0,32},{32,0},{1,33},{33,1},{2,34},{34,2},{3,35},{35,3},{4,36},{36... | collective-permute-start | bytes 1572872 | tf_op jit(solution)/shard_map/ppermute | solution.py:269
  117.8 14.5 %all-to-all-start.3 = ((bf16[16,8,2048]{2,1,0:T(8,128)(2,1)}), bf16[16,8,2048]{2,1,0:T(8,128)(2,1)S(1)}, u32[]{:S(2)}, u32[]{:S(2)}) async-start(bf16[16,8,2048]{2,1,0:T(8,128)(2,1)} %fusion), calls=%async_computation.3 | async-start | bytes 1048576 | tf_op jit(solution)/shard_map/all_to_all | solution.py:265
  121.4 3.4 %collective-permute-start.2 = (bf16[128,1024]{1,0:T(8,128)(2,1)S(1)}, bf16[128,1024]{1,0:T(8,128)(2,1)S(1)}, u32[]{:S(2)}, u32[]{:S(2)}) collective-permute-start(bf16[128,1024]{1,0:T(8,128)(2,1)S(1)} %copy-done.10), channel_id=1, source_target_pairs={{0,32},{32,0},{1,33},{33,1},{2,34},{34,2},{3,35},{35,3},{4,36},{36... | collective-permute-start | bytes 786440 | tf_op jit(solution)/shard_map/ppermute | solution.py:269
  124.8 0.7 copy-start.7
  132.3 0.8 copy-start.2
Sparse Core Ops, SparseCore 0:
  16.7 72.3 all-gather.1
